TPU v7x, 32 devices: a whole 2x2x4 slice. The times are simulated.
32 devices in a mesh: gx: 4 (over z), gy: 8 (over y, x, core).
Axes of the slice: x: 2, y: 2, z: 4, core: 2. Of those that a mesh axis runs over, the one named last changes fastest.
Arguments:
- initial_field: float32 [8, 32, 2048], P(None, 'gx', 'gy'), may hold values from -6 to 6
- target_field: float32 [8, 32, 2048], P(None, 'gx', 'gy'), may hold values from -8 to 8
- land_mask: int32 [32, 2048], P('gx', 'gy'), may hold values 0 or 1
- conv_one: float32 [64, 73], replicated, may hold values from -0.75 to 0.75
- conv_two: float32 [64, 577], replicated, may hold values from -0.25 to 0.25
- head_weights: float32 [32, 65], replicated, may hold values from -0.75 to 0.75
- dir_one: float32 [64, 73], replicated, may hold values from -6 to 6
- dir_two: float32 [64, 577], replicated, may hold values from -6 to 6
- dir_three: float32 [32, 65], replicated, may hold values from -6 to 6
- group_ids: int32 [160], replicated, may hold values from 0 to 5, as said below
Outputs:
- final_field: float32 [8, 32, 2048], P(None, 'gx', 'gy')
- update_one: float32 [64, 73], replicated
- update_two: float32 [64, 577], replicated
- update_three: float32 [32, 65], replicated
Inputs may be any that keep to these rules, and one draw needn't show every extreme that they name: `group_ids`: each of the 6 group numbers names 26 or 27 rows.
All inputs are finite; a program needn't handle non-finite values. No bound on the sum of `land_mask` on one device may be relied on, other than what follows from the above.
Results may differ from a plain program's by a relative error of at most 0.0024.
The roundings to bfloat16 on the way count: a program that leaves them out, or rounds other values in their place, can miss the bound.
Values may be sent and summed in bfloat16 or wider, within the bound.
A program may use at most 64 MiB of HBM per device.

v0:
```python
import functools
import math

import jax
import jax.numpy as jnp
from jax import lax
from jax.experimental import pallas as pl
from jax.experimental.pallas import tpu as pltpu
from jax.sharding import PartitionSpec as P

GROUPS = 6
PARAMS = 43680
RIM = 6
NEAR = 2
LEV = 8
C = 64
K = 32
TILE = 128
MESH = pl.DeviceIdType.MESH
F32 = jnp.float32
BF16 = jnp.bfloat16
VM = pl.BlockSpec(memory_space=pltpu.VMEM)
LIMIT = 56 * 1024 * 1024
NT = (((1,), (1,)), ((), ()))


def dot(a, b):
    return jnp.dot(a, b, preferred_element_type=F32)


def dot_nt(a, b):
    return lax.dot_general(a, b, NT, preferred_element_type=F32)


def sigmoid(v):
    return 0.5 * jnp.tanh(0.5 * v) + 0.5


def halo_kernel(sizes, field, target, mask, fld, tgt, wet, left, right, packed, send_sem, recv_sem):
    n_gx, n_gy = sizes
    gx = lax.axis_index("gx")
    gy = lax.axis_index("gy")
    h, width = mask.shape
    lane = lax.broadcasted_iota(jnp.int32, (3 * LEV, TILE), 1)
    strips = [jnp.zeros((3 * LEV, TILE), F32) for _ in range(2)]
    for r in range(h):
        wide_wet = jnp.broadcast_to(mask[r : r + 1, :].astype(F32), (LEV, width))
        values = wide_wet * field[:, r, :]
        goal = target[:, r, :]
        fld[RIM + r] = values
        tgt[NEAR + r] = goal
        rows = jnp.concatenate([values, wide_wet, goal], axis=0)
        here = (lane >= LEV * r) & (lane < LEV * r + LEV)
        low = rows[:, :TILE]
        high = rows[:, width - TILE :]
        strips[0] = jnp.where(here, roll(high, LEV * r + LEV), strips[0])
        strips[1] = jnp.where(here, roll(low, LEV * r), strips[1])
    wet[1] = mask[...].astype(F32)
    packed[0] = strips[0]
    packed[1] = strips[1]

    moves = [(dx, dy) for dx in (-1, 0, 1) for dy in (-1, 0, 1) if (dx, dy) != (0, 0)]

    def exists(dx, dy):
        x = gx + dx
        y = gy + dy
        return (x >= 0) & (x < n_gx) & (y >= 0) & (y < n_gy)

    def pairs(dx, dy):
        if dy:
            side = left if dy > 0 else right
            return [(packed.at[0 if dy > 0 else 1], side.at[1 - dx])]
        if dx > 0:
            return [
                (fld.at[pl.ds(h, RIM)], fld.at[pl.ds(0, RIM)]),
                (tgt.at[pl.ds(h, NEAR)], tgt.at[pl.ds(0, NEAR)]),
                (wet.at[1], wet.at[0]),
            ]
        return [
            (fld.at[pl.ds(RIM, RIM)], fld.at[pl.ds(RIM + h, RIM)]),
            (tgt.at[pl.ds(NEAR, NEAR)], tgt.at[pl.ds(NEAR + h, NEAR)]),
            (wet.at[1], wet.at[2]),
        ]

    barrier = pltpu.get_barrier_semaphore()
    count = jnp.int32(0)
    for dx, dy in moves:
        @pl.when(exists(dx, dy))
        def _():
            pl.semaphore_signal(barrier, inc=1, device_id=(gx + dx, gy + dy), device_id_type=MESH)
        count = count + jnp.where(exists(dx, dy), 1, 0)
    for dx, dy in moves:
        @pl.when(jnp.logical_not(exists(-dx, -dy)))
        def _():
            for _, dst in pairs(dx, dy):
                dst[...] = jnp.zeros(dst.shape, F32)
    pl.semaphore_wait(barrier, count)

    copies = []
    index = 0
    for dx, dy in moves:
        group = []
        for src, dst in pairs(dx, dy):
            group.append(
                pltpu.make_async_remote_copy(
                    src_ref=src,
                    dst_ref=dst,
                    send_sem=send_sem.at[index],
                    recv_sem=recv_sem.at[index],
                    device_id=(gx + dx, gy + dy),
                    device_id_type=MESH,
                )
            )
            index += 1
        copies.append((dx, dy, group))
    for dx, dy, group in copies:
        @pl.when(exists(dx, dy))
        def _():
            for copy in group:
                copy.start()
    for dx, dy, group in copies:
        @pl.when(exists(-dx, -dy))
        def _():
            for copy in group:
                copy.wait_recv()
    for dx, dy, group in copies:
        @pl.when(exists(dx, dy))
        def _():
            for copy in group:
                copy.wait_send()


def roll(v, shift):
    return pltpu.roll(v, shift % v.shape[1], 1)


def compute_kernel(
    sizes, own, goal, mask, left, right, w1_ref, w2_ref, w3_ref,
    final_ref, grads_ref,
    fld, wet_s, tgt, adj, x9, z1, h1, z2, h2, prob, e2m, up, e1m, vv, e3m,
):
    n_gx, n_gy = sizes
    gx = lax.axis_index("gx")
    gy = lax.axis_index("gy")
    rows, _, width = own.shape
    h = rows - 2 * RIM
    wide = width + TILE

    is_right = lax.broadcasted_iota(jnp.int32, (3 * LEV, TILE), 1) < TILE // 2

    for r in range(rows):
        where = 0 if r < RIM else 1 if r < RIM + h else 2
        k = (r + h - RIM) % h
        rest = jnp.where(
            is_right, roll(right[where], -LEV * k), roll(left[where], -LEV * k - LEV)
        )
        fld[0, r] = jnp.concatenate([own[r], rest[:LEV]], axis=1)
        wet_row = jnp.broadcast_to(mask[where, k : k + 1, :], (LEV, width))
        wet_s[r] = jnp.concatenate([wet_row, rest[LEV : 2 * LEV]], axis=1)
        if RIM - NEAR <= r < RIM + h + NEAR:
            tgt[r] = jnp.concatenate([goal[r - RIM + NEAR], rest[2 * LEV :]], axis=1)

    wa = w1_ref[...]
    w1 = wa[:, : 9 * LEV].astype(BF16)
    b1 = wa[:, 9 * LEV :]
    wb = w2_ref[...]
    tap = lambda a, b: wb[:, (3 * a + b) * C : (3 * a + b + 1) * C]
    w2f = jnp.concatenate(
        [jnp.concatenate([tap(a, b) for a in range(3)], axis=1) for b in range(3)], axis=0
    )
    w2 = w2f.astype(BF16)
    w2t = w2f.T.astype(BF16)
    b2 = wb[:, 9 * C :]
    wc = w3_ref[...]
    w3 = wc[:, :C].astype(BF16)
    w3t = wc[:, :C].T.astype(BF16)
    b3 = wc[:, C:]
    w1t = wa[:, : 9 * LEV].T.astype(BF16)

    col_left = jnp.where(gy > 0, 1.0, 0.0).astype(F32)
    col_right = jnp.where(gy < n_gy - 1, 1.0, 0.0).astype(F32)
    side = jnp.where(is_right[0:1], col_right, col_left)
    col_ok = jnp.concatenate([jnp.ones((1, width), F32), side], axis=1)

    def inside(r):
        i = gx * h + r - RIM
        ok = (i >= 0) & (i < n_gx * h)
        return col_ok * jnp.where(ok, 1.0, 0.0).astype(F32)

    def loop(start, stop, body):
        lax.fori_loop(start, stop, lambda r, c: (body(r), c)[1], 0, unroll=True)

    def forward(s, rad):
        def first(r):
            parts = []
            for a in range(3):
                row = fld[s, r + a - 1]
                parts += [roll(row, 1), row, roll(row, -1)]
            cols = jnp.concatenate(parts, axis=0).astype(BF16)
            x9[s, r] = cols
            z = dot(w1, cols) + b1
            z1[s, r] = z
            h1[s, r] = (z * sigmoid(z) * inside(r)).astype(BF16)

        loop(RIM - rad - 1, RIM + h + rad + 1, first)

        def second(r):
            h3 = jnp.concatenate([h1[s, r - 1], h1[s, r], h1[s, r + 1]], axis=0)
            y = dot(w2, h3)
            z = roll(y[0:C], 1) + y[C : 2 * C] + roll(y[2 * C :], -1) + b2
            z2[s, r] = z
            hb = (z * sigmoid(z)).astype(BF16)
            h2[s, r] = hb
            p = sigmoid(dot(w3, hb) + b3)
            prob[s, r] = p
            center = fld[s, r]
            c = 0.25 * p
            change = (
                c[0:8] * (fld[s, r + 1] - center)
                + c[8:16] * (fld[s, r - 1] - center)
                + c[16:24] * (roll(center, -1) - center)
                + c[24:32] * (roll(center, 1) - center)
            )
            fld[s + 1, r] = center + wet_s[r] * change

        loop(RIM - rad, RIM + h + rad, second)

    forward(0, 4)
    forward(1, 2)
    for r in range(h):
        final_ref[:, r, :] = fld[2, RIM + r][:, :width]

    def adjoint_start(r):
        adj[1, r] = wet_s[r] * (fld[2, r] - tgt[r])

    loop(RIM - 2, RIM + h + 2, adjoint_start)

    lane_w = lax.broadcasted_iota(jnp.int32, (1, wide), 1)
    own_lane = jnp.where(lane_w < width, 1.0, 0.0).astype(F32)
    fold = lambda v: sum(v[:, k * TILE : (k + 1) * TILE] for k in range(v.shape[1] // TILE))

    def errors(s, r):
        center = fld[s, r]
        wg = wet_s[r] * adj[s, r]
        p = prob[s, r]
        diff = jnp.concatenate(
            [
                wg * (fld[s, r + 1] - center),
                wg * (fld[s, r - 1] - center),
                wg * (roll(center, -1) - center),
                wg * (roll(center, 1) - center),
            ],
            axis=0,
        )
        e3 = diff * (0.25 * p * (1.0 - p))
        e3b = e3.astype(BF16)
        z = z2[s, r]
        g = sigmoid(z)
        e2 = dot(w3t, e3b) * (g * (1.0 + z * (1.0 - g)))
        return e3, e3b, e2

    def spread(e2):
        return jnp.concatenate([roll(e2, -1), e2, roll(e2, 1)], axis=0).astype(BF16)

    zero_b = (jnp.zeros((K, TILE), F32), jnp.zeros((C, TILE), F32))

    def own_rows(s, carry):
        def body(r, c):
            e3, e3b, e2 = errors(s, r)
            e3m[s, r - RIM] = e3b[:, :width]
            em = e2 * own_lane
            m = spread(em)
            e2m[s, r - RIM] = m
            if s == 0:
                up[r] = dot(w2t, m)
            else:
                up[r] = dot(w2t, spread(e2))
            return (c[0] + fold(e3[:, :width]), c[1] + fold(e2[:, :width]))

        return lax.fori_loop(RIM, RIM + h, body, carry, unroll=True)

    def rim_row(r):
        _, _, e2 = errors(1, r)
        up[r] = dot(w2t, spread(e2))

    def first_error(s, r):
        hid = up[r + 1][0:C] + up[r][C : 2 * C] + up[r - 1][2 * C :]
        z = z1[s, r]
        g = sigmoid(z)
        return hid * (g * (1.0 + z * (1.0 - g))) * inside(r)

    sums = own_rows(1, zero_b)
    for r in (RIM - 2, RIM - 1, RIM + h, RIM + h + 1):
        rim_row(r)

    def back_one(r, c):
        e1 = first_error(1, r)
        eb = e1.astype(BF16)
        e1m[1, r - RIM + 1] = (e1 * own_lane).astype(BF16)
        t = dot(w1t, eb)
        piece = lambda a, b: t[(3 * a + b) * LEV : (3 * a + b + 1) * LEV]
        for a in range(3):
            vv[r, a] = roll(piece(a, 0), -1) + piece(a, 1) + roll(piece(a, 2), 1)
        keep = jnp.where((r >= RIM) & (r < RIM + h), 1.0, 0.0).astype(F32)
        return c + fold(e1[:, :width]) * keep

    sum_one = lax.fori_loop(
        RIM - 1, RIM + h + 1, back_one, jnp.zeros((C, TILE), F32), unroll=True
    )

    def adjoint_next(r):
        wg = wet_s[r] * adj[1, r]
        p = prob[1, r]
        c = [0.25 * p[n * 8 : n * 8 + 8] for n in range(4)]
        above = wet_s[r - 1] * adj[1, r - 1] * (0.25 * prob[1, r - 1][0:8])
        below = wet_s[r + 1] * adj[1, r + 1] * (0.25 * prob[1, r + 1][8:16])
        adj[0, r] = (
            adj[1, r]
            - wg * (c[0] + c[1] + c[2] + c[3])
            + above
            + below
            + roll(wg * c[2], 1)
            + roll(wg * c[3], -1)
            + vv[r + 1, 0]
            + vv[r, 1]
            + vv[r - 1, 2]
        )

    loop(RIM, RIM + h, adjoint_next)

    sums = own_rows(0, sums)
    for r in (RIM - 2, RIM - 1, RIM + h, RIM + h + 1):
        up[r] = jnp.zeros((3 * C, wide), F32)

    def back_zero(r, c):
        e1 = first_error(0, r)
        e1m[0, r - RIM + 1] = e1.astype(BF16)
        return c + fold(e1)

    sum_one = lax.fori_loop(RIM - 1, RIM + h + 1, back_zero, sum_one, unroll=True)

    g1 = jnp.zeros((C, 9 * LEV), F32)
    g2 = jnp.zeros((3 * C, 3 * C), F32)
    g3 = jnp.zeros((K, C), F32)
    for s in range(2):
        for r in range(h):
            h3 = jnp.concatenate([h1[s, RIM + r + a - 1] for a in range(3)], axis=0)
            g2 = g2 + dot_nt(e2m[s, r], h3)
            g3 = g3 + dot_nt(e3m[s, r], h2[s, RIM + r][:, :width])
        for r in range(h + 2) if s == 0 else range(1, h + 1):
            g1 = g1 + dot_nt(e1m[s, r], x9[s, RIM + r - 1])
    total = lambda v: jnp.sum(v, axis=1, keepdims=True)
    pad = lambda v: jnp.concatenate([v, jnp.zeros((v.shape[0], C - v.shape[1]), F32)], axis=1)
    extra = jnp.concatenate(
        [
            g1[:, :C],
            pad(jnp.concatenate([g1[:, C:], total(sum_one), total(sums[1])], axis=1)),
            g3,
            pad(total(sums[0])),
        ],
        axis=0,
    )
    grads_ref[: 3 * C, :] = jnp.concatenate([g2, extra], axis=1)
    spare = grads_ref.shape[0] - 3 * C
    if spare:
        grads_ref[3 * C :, :] = jnp.zeros((spare, 4 * C), F32)


def sum_kernel(sizes, grads, out, got, part, parts, send_one, recv_one, send_two, recv_two,
               send_three, recv_three):
    n_gx, n_gy = sizes
    gx = lax.axis_index("gx")
    gy = lax.axis_index("gy")
    chunk = grads.shape[0] // n_gy
    barrier = pltpu.get_barrier_semaphore()
    ys = [lax.rem(gy + k, n_gy) for k in range(1, n_gy)]
    xs = [lax.rem(gx + k, n_gx) for k in range(1, n_gx)]
    for y in ys:
        pl.semaphore_signal(barrier, inc=1, device_id=(gx, y), device_id_type=MESH)
    for x in xs:
        pl.semaphore_signal(barrier, inc=1, device_id=(x, gy), device_id_type=MESH)
    pl.semaphore_wait(barrier, n_gy + n_gx - 2)

    def rows(y):
        return pl.ds(pl.multiple_of(y * chunk, 8), chunk)

    one = [
        pltpu.make_async_remote_copy(
            src_ref=grads.at[rows(y)], dst_ref=got.at[k],
            send_sem=send_one.at[k], recv_sem=recv_one.at[k],
            device_id=(gx, y), device_id_type=MESH,
        )
        for k, y in enumerate(ys)
    ]
    for copy in one:
        copy.start()
    acc = grads[rows(gy), :]
    for k, copy in enumerate(one):
        copy.wait_recv()
        acc = acc + got[k]
    part[...] = acc
    two = [
        pltpu.make_async_remote_copy(
            src_ref=part, dst_ref=parts.at[gx],
            send_sem=send_two.at[k], recv_sem=recv_two.at[k],
            device_id=(x, gy), device_id_type=MESH,
        )
        for k, x in enumerate(xs)
    ]
    for copy in two:
        copy.start()
    parts[gx] = acc
    for copy in two:
        copy.wait_recv()
    acc = parts[0]
    for x in range(1, n_gx):
        acc = acc + parts[x]
    out[rows(gy), :] = acc
    three = [
        pltpu.make_async_remote_copy(
            src_ref=out.at[rows(gy)], dst_ref=out.at[rows(gy)],
            send_sem=send_three.at[k], recv_sem=recv_three.at[k],
            device_id=(gx, y), device_id_type=MESH,
        )
        for k, y in enumerate(ys)
    ]
    for copy in three:
        copy.start()
    for copy in three:
        copy.wait_recv()
    for copy in one + two + three:
        copy.wait_send()


def finish_kernel(grads, d1, d2, d3, ids, u1, u2, u3):
    g = grads[: 3 * C, :]
    block = lambda a, b: g[b * C : (b + 1) * C, a * C : (a + 1) * C]
    side = g[:, 3 * C :]
    one = jnp.concatenate([side[:C], side[C : 2 * C, : 9 * LEV - C + 1]], axis=1)
    bias_two = side[C : 2 * C, 9 * LEV - C + 1 : 9 * LEV - C + 2]
    two = jnp.concatenate([block(a, b) for a in range(3) for b in range(3)] + [bias_two], axis=1)
    three = jnp.concatenate([side[2 * C : 2 * C + K], side[2 * C + K :, 0:1]], axis=1)
    members = [one, two, three]
    heads = [d1[...], d2[...], d3[...]]
    row_sq = lambda v: jnp.sum(v * v, axis=1, keepdims=True)
    grad_rows = jnp.concatenate([row_sq(m) for m in members], axis=0)
    dir_rows = jnp.concatenate([row_sq(m) for m in heads], axis=0)
    total = jnp.sum(grad_rows, axis=0, keepdims=True)
    factor = 1.0 / jnp.maximum(jnp.sqrt(total), 1.0)
    clip_rows = grad_rows * (factor * factor)
    count = grad_rows.shape[0]
    i0 = lax.broadcasted_iota(jnp.int32, (count, count), 0)
    i1 = lax.broadcasted_iota(jnp.int32, (count, count), 1)
    spread = jnp.broadcast_to(ids[...].astype(F32), (count, count))
    column = jnp.sum(jnp.where(i0 == i1, spread, 0.0), axis=1, keepdims=True)
    row_ratio = jnp.zeros((count, 1), F32)
    for k in range(GROUPS):
        hit = column == float(k)
        pick = lambda v: jnp.sum(jnp.where(hit, v, 0.0), axis=0, keepdims=True)
        ratio = jnp.sqrt(pick(clip_rows)) / jnp.sqrt(pick(dir_rows) + 1e-06)
        row_ratio = row_ratio + jnp.where(hit, ratio, 0.0)
    scaling = math.sqrt(PARAMS)
    start = 0
    for ref, member, head in zip((u1, u2, u3), members, heads):
        n = member.shape[0]
        ref[...] = scaling * (member * factor + row_ratio[start : start + n] * head)
        start += n


def per_device(sizes, field, target, mask, conv_one, conv_two, head, d1, d2, d3, ids):
    n_gx, n_gy = sizes
    _, h, width = field.shape
    rows = h + 2 * RIM
    wide = width + TILE
    shape = jax.ShapeDtypeStruct
    chunk = 8 * -(-3 * C // (8 * n_gy))
    own, goal, wet, left, right = pl.pallas_call(
        functools.partial(halo_kernel, sizes),
        name="halo",
        out_shape=[
            shape((rows, LEV, width), F32),
            shape((h + 2 * NEAR, LEV, width), F32),
            shape((3, h, width), F32),
            shape((3, 3 * LEV, TILE), F32),
            shape((3, 3 * LEV, TILE), F32),
        ],
        in_specs=[VM] * 3,
        out_specs=[VM] * 5,
        scratch_shapes=[
            pltpu.VMEM((2, 3 * LEV, TILE), F32),
            pltpu.SemaphoreType.DMA((12,)),
            pltpu.SemaphoreType.DMA((12,)),
        ],
        compiler_params=pltpu.CompilerParams(collective_id=0, has_side_effects=True),
    )(field, target, mask)
    final, grads = pl.pallas_call(
        functools.partial(compute_kernel, sizes),
        name="local",
        out_shape=[shape(field.shape, F32), shape((chunk * n_gy, 4 * C), F32)],
        in_specs=[VM] * 8,
        out_specs=[VM] * 2,
        scratch_shapes=[
            pltpu.VMEM((3, rows, LEV, wide), F32),
            pltpu.VMEM((rows, LEV, wide), F32),
            pltpu.VMEM((rows, LEV, wide), F32),
            pltpu.VMEM((2, rows, LEV, wide), F32),
            pltpu.VMEM((2, rows, 9 * LEV, wide), BF16),
            pltpu.VMEM((2, rows, C, wide), F32),
            pltpu.VMEM((2, rows, C, wide), BF16),
            pltpu.VMEM((2, rows, C, wide), F32),
            pltpu.VMEM((2, rows, C, wide), BF16),
            pltpu.VMEM((2, rows, K, wide), F32),
            pltpu.VMEM((2, h, 3 * C, wide), BF16),
            pltpu.VMEM((rows, 3 * C, wide), F32),
            pltpu.VMEM((2, h + 2, C, wide), BF16),
            pltpu.VMEM((rows, 3, LEV, wide), F32),
            pltpu.VMEM((2, h, K, width), BF16),
        ],
        compiler_params=pltpu.CompilerParams(vmem_limit_bytes=LIMIT),
    )(own, goal, wet, left, right, conv_one, conv_two, head)
    dma = pltpu.SemaphoreType.DMA
    summed = pl.pallas_call(
        functools.partial(sum_kernel, sizes),
        name="gradsum",
        out_shape=shape(grads.shape, F32),
        in_specs=[VM],
        out_specs=VM,
        scratch_shapes=[
            pltpu.VMEM((n_gy - 1, chunk, 4 * C), F32),
            pltpu.VMEM((chunk, 4 * C), F32),
            pltpu.VMEM((n_gx, chunk, 4 * C), F32),
            dma((n_gy - 1,)), dma((n_gy - 1,)),
            dma((n_gx - 1,)), dma((n_gx - 1,)),
            dma((n_gy - 1,)), dma((n_gy - 1,)),
        ],
        compiler_params=pltpu.CompilerParams(collective_id=1, has_side_effects=True),
    )(grads)
    u1, u2, u3 = pl.pallas_call(
        finish_kernel,
        name="update",
        out_shape=[shape(conv_one.shape, F32), shape(conv_two.shape, F32), shape(head.shape, F32)],
        in_specs=[VM] * 5,
        out_specs=[VM] * 3,
    )(summed, d1, d2, d3, ids.reshape(1, -1))
    return final, u1, u2, u3


def solution(mesh):
    grid = P(None, "gx", "gy")
    placed = (grid, grid, P("gx", "gy")) + (P(),) * 7
    return jax.shard_map(
        functools.partial(per_device, (mesh.shape["gx"], mesh.shape["gy"])),
        mesh=mesh,
        in_specs=placed,
        out_specs=(grid, P(), P(), P()),
        check_vma=False,
    )
```

profile of v0, /device:TPU:0, one launch (start us, length us, event | category | flops | bytes accessed | tf_op | source)
XLA Modules:
  0.0 49.3 jit_solution(12782961995519433242)
XLA Ops:
  0.6 9.3 %halo.1 = (f32[20,8,256]{2,1,0:T(8,128)}, f32[12,8,256]{2,1,0:T(8,128)}, f32[3,8,256]{2,1,0:T(8,128)}, f32[3,24,128]{2,1,0:T(8,128)}, f32[3,24,128]{2,1,0:T(8,128)}) custom-call(f32[8,8,256]{2,1,0:T(8,128)} %field.1, f32[8,8,256]{2,1,0:T(8,128)} %target.1, s32[8,256]{1,0:T(8,128)} %mask.1), custom_call_target="tpu_custom_call" | custom-call | tf_op jit(solution)/shard_map/halo/pallas_call | solution.py:477
  10.0 19.5 %local.1 = (f32[8,8,256]{2,1,0:T(8,128)}, f32[192,256]{1,0:T(8,128)}) custom-call(f32[20,8,256]{2,1,0:T(8,128)} %get-tuple-element.14.own, f32[12,8,256]{2,1,0:T(8,128)} %get-tuple-element.15.goal, f32[3,8,256]{2,1,0:T(8,128)} %get-tuple-element.16.mask, f32[3,24,128]{2,1,0:T(8,128)} %get-tuple-element.17.left, f32[3,24,128]{2,1,0:T(8,128)} %get-tuple-element.18.right, ...), custom_call_target="tpu_custom_call" | custom-call | tf_op jit(solution)/shard_map/local/pallas_call | solution.py:496
  29.4 17.6 %gradsum.1.grads = f32[192,256]{1,0:T(8,128)} custom-call(f32[192,256]{1,0:T(8,128)} %get-tuple-element.20.grads), custom_call_target="tpu_custom_call" | custom-call | tf_op jit(solution)/shard_map/gradsum/pallas_call | solution.py:522
  47.1 2.2 %update.1 = (f32[64,73]{1,0:T(8,128)}, f32[64,577]{1,0:T(8,128)}, f32[32,65]{1,0:T(8,128)}) custom-call(f32[192,256]{1,0:T(8,128)} %gradsum.1.grads, f32[64,73]{1,0:T(8,128)} %d1.1, f32[64,577]{1,0:T(8,128)} %d2.1, f32[32,65]{1,0:T(8,128)} %d3.1, s32[1,160]{1,0:T(1,128)} %bitcast.1), custom_call_target="tpu_custom_call" | custom-call | tf_op jit(solution)/shard_map/update/pallas_call | solution.py:538
where the time goes:
time: 49.5 us; the launch traced here: 49.3 us
  Pallas kernels  48.6 us (98%)
  between operations  0.65 us (1%)
    pallas_call x1, Pallas kernels, per_device(): pl.pallas_call(functools.partial(compute_kernel, sizes), name='local', ou...  19.5 us
    pallas_call x1, Pallas kernels, per_device(): pl.pallas_call(functools.partial(sum_kernel, sizes), name='gradsum', out_...  17.6 us
    pallas_call x1, Pallas kernels, per_device(): pl.pallas_call(functools.partial(halo_kernel, sizes), name='halo', out_sh...  9.35 us
    pallas_call x1, Pallas kernels, per_device(): pl.pallas_call(finish_kernel, name='update', out_shape=[shape(conv_one.sh...  2.19 us

commit v1 on v0

--- a/solution.py
+++ b/solution.py
@@ -20,6 +20,7 @@
 F32 = jnp.float32
 BF16 = jnp.bfloat16
 VM = pl.BlockSpec(memory_space=pltpu.VMEM)
+ANY = pl.BlockSpec(memory_space=pl.ANY)
 LIMIT = 56 * 1024 * 1024
 NT = (((1,), (1,)), ((), ()))
 
@@ -36,64 +37,99 @@
     return 0.5 * jnp.tanh(0.5 * v) + 0.5
 
 
-def halo_kernel(sizes, field, target, mask, fld, tgt, wet, left, right, packed, send_sem, recv_sem):
+def roll(v, shift):
+    return pltpu.roll(v, shift % v.shape[1], 1)
+
+
+def fused_kernel(
+    sizes, field_in, target_in, mask_in, w1_in, w2_in, w3_in,
+    final_ref, out_ref,
+    fld, wet_s, tgt, adj, x9, z1, h1, z2, h2, prob, e2m, up, e1m, vv, e3m,
+    field, target, mask, w1_ref, w2_ref, w3_ref, wet, left, right, packed,
+    grads_ref, got, part, parts, mine,
+    load_sem, send_sem, recv_sem, send_one, recv_one, send_two, recv_two, send_three, recv_three,
+):
     n_gx, n_gy = sizes
     gx = lax.axis_index("gx")
     gy = lax.axis_index("gy")
     h, width = mask.shape
+    rows = h + 2 * RIM
+    wide = width + TILE
+    ys = [lax.rem(gy + k, n_gy) for k in range(1, n_gy)]
+    xs = [lax.rem(gx + k, n_gx) for k in range(1, n_gx)]
+    moves = [(dx, dy) for dx in (-1, 0, 1) for dy in (-1, 0, 1) if (dx, dy) != (0, 0)]
+
+    def exists(dx, dy):
+        x = gx + dx
+        y = gy + dy
+        return (x >= 0) & (x < n_gx) & (y >= 0) & (y < n_gy)
+
+    barrier = pltpu.get_barrier_semaphore()
+    count = jnp.int32(n_gy + n_gx - 2)
+    for dx, dy in moves:
+        if dx and dy:
+            @pl.when(exists(dx, dy))
+            def _():
+                pl.semaphore_signal(barrier, inc=1, device_id=(gx + dx, gy + dy), device_id_type=MESH)
+            count = count + jnp.where(exists(dx, dy), 1, 0)
+    for x in xs:
+        pl.semaphore_signal(barrier, inc=1, device_id=(x, gy), device_id_type=MESH)
+    for y in ys:
+        pl.semaphore_signal(barrier, inc=1, device_id=(gx, y), device_id_type=MESH)
+
+    loads = [
+        pltpu.make_async_copy(src, dst, load_sem.at[i])
+        for i, (src, dst) in enumerate(
+            [(field_in, field), (target_in, target), (mask_in, mask),
+             (w1_in, w1_ref), (w2_in, w2_ref), (w3_in, w3_ref)]
+        )
+    ]
+    for copy in loads:
+        copy.start()
+
+    def pairs(dx, dy):
+        if dy:
+            side = left if dy > 0 else right
+            return [(packed.at[0 if dy > 0 else 1], side.at[1 - dx])]
+        near = pl.ds(0, width)
+        if dx > 0:
+            return [
+                (fld.at[0, pl.ds(h, RIM), :, near], fld.at[0, pl.ds(0, RIM), :, near]),
+                (tgt.at[pl.ds(RIM + h - NEAR, NEAR), :, near], tgt.at[pl.ds(RIM - NEAR, NEAR), :, near]),
+                (wet.at[1], wet.at[0]),
+            ]
+        return [
+            (fld.at[0, pl.ds(RIM, RIM), :, near], fld.at[0, pl.ds(RIM + h, RIM), :, near]),
+            (tgt.at[pl.ds(RIM, NEAR), :, near], tgt.at[pl.ds(RIM + h, NEAR), :, near]),
+            (wet.at[1], wet.at[2]),
+        ]
+
+    for dx, dy in moves:
+        @pl.when(jnp.logical_not(exists(-dx, -dy)))
+        def _():
+            for _, dst in pairs(dx, dy):
+                dst[...] = jnp.zeros(dst.shape, F32)
+
+    for copy in loads[:3]:
+        copy.wait()
     lane = lax.broadcasted_iota(jnp.int32, (3 * LEV, TILE), 1)
     strips = [jnp.zeros((3 * LEV, TILE), F32) for _ in range(2)]
     for r in range(h):
         wide_wet = jnp.broadcast_to(mask[r : r + 1, :].astype(F32), (LEV, width))
         values = wide_wet * field[:, r, :]
         goal = target[:, r, :]
-        fld[RIM + r] = values
-        tgt[NEAR + r] = goal
-        rows = jnp.concatenate([values, wide_wet, goal], axis=0)
+        fld[0, RIM + r, :, :width] = values
+        tgt[RIM + r, :, :width] = goal
+        mixed = jnp.concatenate([values, wide_wet, goal], axis=0)
         here = (lane >= LEV * r) & (lane < LEV * r + LEV)
-        low = rows[:, :TILE]
-        high = rows[:, width - TILE :]
+        low = mixed[:, :TILE]
+        high = mixed[:, width - TILE :]
         strips[0] = jnp.where(here, roll(high, LEV * r + LEV), strips[0])
         strips[1] = jnp.where(here, roll(low, LEV * r), strips[1])
     wet[1] = mask[...].astype(F32)
     packed[0] = strips[0]
     packed[1] = strips[1]
 
-    moves = [(dx, dy) for dx in (-1, 0, 1) for dy in (-1, 0, 1) if (dx, dy) != (0, 0)]
-
-    def exists(dx, dy):
-        x = gx + dx
-        y = gy + dy
-        return (x >= 0) & (x < n_gx) & (y >= 0) & (y < n_gy)
-
-    def pairs(dx, dy):
-        if dy:
-            side = left if dy > 0 else right
-            return [(packed.at[0 if dy > 0 else 1], side.at[1 - dx])]
-        if dx > 0:
-            return [
-                (fld.at[pl.ds(h, RIM)], fld.at[pl.ds(0, RIM)]),
-                (tgt.at[pl.ds(h, NEAR)], tgt.at[pl.ds(0, NEAR)]),
-                (wet.at[1], wet.at[0]),
-            ]
-        return [
-            (fld.at[pl.ds(RIM, RIM)], fld.at[pl.ds(RIM + h, RIM)]),
-            (tgt.at[pl.ds(NEAR, NEAR)], tgt.at[pl.ds(NEAR + h, NEAR)]),
-            (wet.at[1], wet.at[2]),
-        ]
-
-    barrier = pltpu.get_barrier_semaphore()
-    count = jnp.int32(0)
-    for dx, dy in moves:
-        @pl.when(exists(dx, dy))
-        def _():
-            pl.semaphore_signal(barrier, inc=1, device_id=(gx + dx, gy + dy), device_id_type=MESH)
-        count = count + jnp.where(exists(dx, dy), 1, 0)
-    for dx, dy in moves:
-        @pl.when(jnp.logical_not(exists(-dx, -dy)))
-        def _():
-            for _, dst in pairs(dx, dy):
-                dst[...] = jnp.zeros(dst.shape, F32)
     pl.semaphore_wait(barrier, count)
 
     copies = []
@@ -118,48 +154,9 @@
         def _():
             for copy in group:
                 copy.start()
-    for dx, dy, group in copies:
-        @pl.when(exists(-dx, -dy))
-        def _():
-            for copy in group:
-                copy.wait_recv()
-    for dx, dy, group in copies:
-        @pl.when(exists(dx, dy))
-        def _():
-            for copy in group:
-                copy.wait_send()
-
-
-def roll(v, shift):
-    return pltpu.roll(v, shift % v.shape[1], 1)
-
-
-def compute_kernel(
-    sizes, own, goal, mask, left, right, w1_ref, w2_ref, w3_ref,
-    final_ref, grads_ref,
-    fld, wet_s, tgt, adj, x9, z1, h1, z2, h2, prob, e2m, up, e1m, vv, e3m,
-):
-    n_gx, n_gy = sizes
-    gx = lax.axis_index("gx")
-    gy = lax.axis_index("gy")
-    rows, _, width = own.shape
-    h = rows - 2 * RIM
-    wide = width + TILE
-
-    is_right = lax.broadcasted_iota(jnp.int32, (3 * LEV, TILE), 1) < TILE // 2
-
-    for r in range(rows):
-        where = 0 if r < RIM else 1 if r < RIM + h else 2
-        k = (r + h - RIM) % h
-        rest = jnp.where(
-            is_right, roll(right[where], -LEV * k), roll(left[where], -LEV * k - LEV)
-        )
-        fld[0, r] = jnp.concatenate([own[r], rest[:LEV]], axis=1)
-        wet_row = jnp.broadcast_to(mask[where, k : k + 1, :], (LEV, width))
-        wet_s[r] = jnp.concatenate([wet_row, rest[LEV : 2 * LEV]], axis=1)
-        if RIM - NEAR <= r < RIM + h + NEAR:
-            tgt[r] = jnp.concatenate([goal[r - RIM + NEAR], rest[2 * LEV :]], axis=1)
-
+
+    for copy in loads[3:]:
+        copy.wait()
     wa = w1_ref[...]
     w1 = wa[:, : 9 * LEV].astype(BF16)
     b1 = wa[:, 9 * LEV :]
@@ -176,6 +173,25 @@
     w3t = wc[:, :C].T.astype(BF16)
     b3 = wc[:, C:]
     w1t = wa[:, : 9 * LEV].T.astype(BF16)
+
+    is_right = lax.broadcasted_iota(jnp.int32, (3 * LEV, TILE), 1) < TILE // 2
+    for dx, dy, group in copies:
+        @pl.when(exists(-dx, -dy))
+        def _():
+            for copy in group:
+                copy.wait_recv()
+
+    for r in range(rows):
+        where = 0 if r < RIM else 1 if r < RIM + h else 2
+        k = (r + h - RIM) % h
+        side_tile = jnp.where(
+            is_right, roll(right[where], -LEV * k), roll(left[where], -LEV * k - LEV)
+        )
+        fld[0, r, :, width:] = side_tile[:LEV]
+        wet_row = jnp.broadcast_to(wet[where, k : k + 1, :], (LEV, width))
+        wet_s[r] = jnp.concatenate([wet_row, side_tile[LEV : 2 * LEV]], axis=1)
+        if RIM - NEAR <= r < RIM + h + NEAR:
+            tgt[r, :, width:] = side_tile[2 * LEV :]
 
     col_left = jnp.where(gy > 0, 1.0, 0.0).astype(F32)
     col_right = jnp.where(gy < n_gy - 1, 1.0, 0.0).astype(F32)
@@ -360,33 +376,18 @@
         ],
         axis=0,
     )
-    grads_ref[: 3 * C, :] = jnp.concatenate([g2, extra], axis=1)
-    spare = grads_ref.shape[0] - 3 * C
-    if spare:
-        grads_ref[3 * C :, :] = jnp.zeros((spare, 4 * C), F32)
-
-
-def sum_kernel(sizes, grads, out, got, part, parts, send_one, recv_one, send_two, recv_two,
-               send_three, recv_three):
-    n_gx, n_gy = sizes
-    gx = lax.axis_index("gx")
-    gy = lax.axis_index("gy")
-    chunk = grads.shape[0] // n_gy
-    barrier = pltpu.get_barrier_semaphore()
-    ys = [lax.rem(gy + k, n_gy) for k in range(1, n_gy)]
-    xs = [lax.rem(gx + k, n_gx) for k in range(1, n_gx)]
-    for y in ys:
-        pl.semaphore_signal(barrier, inc=1, device_id=(gx, y), device_id_type=MESH)
-    for x in xs:
-        pl.semaphore_signal(barrier, inc=1, device_id=(x, gy), device_id_type=MESH)
-    pl.semaphore_wait(barrier, n_gy + n_gx - 2)
-
-    def rows(y):
-        return pl.ds(pl.multiple_of(y * chunk, 8), chunk)
+    packed_grads = jnp.concatenate([g2, extra], axis=1)
+    chunk = grads_ref.shape[1]
+    for y in range(n_gy):
+        lo = y * chunk
+        if lo + chunk <= 3 * C:
+            grads_ref[y] = packed_grads[lo : lo + chunk]
+        else:
+            grads_ref[y] = jnp.zeros((chunk, 4 * C), F32)
 
     one = [
         pltpu.make_async_remote_copy(
-            src_ref=grads.at[rows(y)], dst_ref=got.at[k],
+            src_ref=grads_ref.at[y], dst_ref=got.at[k],
             send_sem=send_one.at[k], recv_sem=recv_one.at[k],
             device_id=(gx, y), device_id_type=MESH,
         )
@@ -394,7 +395,7 @@
     ]
     for copy in one:
         copy.start()
-    acc = grads[rows(gy), :]
+    acc = grads_ref[gy]
     for k, copy in enumerate(one):
         copy.wait_recv()
         acc = acc + got[k]
@@ -415,10 +416,11 @@
     acc = parts[0]
     for x in range(1, n_gx):
         acc = acc + parts[x]
-    out[rows(gy), :] = acc
+    acc = acc.astype(out_ref.dtype)
+    mine[...] = acc
     three = [
         pltpu.make_async_remote_copy(
-            src_ref=out.at[rows(gy)], dst_ref=out.at[rows(gy)],
+            src_ref=mine, dst_ref=out_ref.at[gy],
             send_sem=send_three.at[k], recv_sem=recv_three.at[k],
             device_id=(gx, y), device_id_type=MESH,
         )
@@ -426,14 +428,22 @@
     ]
     for copy in three:
         copy.start()
+    out_ref[gy] = acc
     for copy in three:
         copy.wait_recv()
+    for dx, dy, group in copies:
+        @pl.when(exists(dx, dy))
+        def _():
+            for copy in group:
+                copy.wait_send()
     for copy in one + two + three:
         copy.wait_send()
 
 
-def finish_kernel(grads, d1, d2, d3, ids, u1, u2, u3):
-    g = grads[: 3 * C, :]
+def finish_kernel(grads, final, d1, d2, d3, ids, final_out, u1, u2, u3):
+    final_out[...] = final[...]
+    n_parts = 3 * C // grads.shape[1]
+    g = jnp.concatenate([grads[y].astype(F32) for y in range(n_parts)], axis=0)
     block = lambda a, b: g[b * C : (b + 1) * C, a * C : (a + 1) * C]
     side = g[:, 3 * C :]
     one = jnp.concatenate([side[:C], side[C : 2 * C, : 9 * LEV - C + 1]], axis=1)
@@ -474,30 +484,12 @@
     wide = width + TILE
     shape = jax.ShapeDtypeStruct
     chunk = 8 * -(-3 * C // (8 * n_gy))
-    own, goal, wet, left, right = pl.pallas_call(
-        functools.partial(halo_kernel, sizes),
-        name="halo",
-        out_shape=[
-            shape((rows, LEV, width), F32),
-            shape((h + 2 * NEAR, LEV, width), F32),
-            shape((3, h, width), F32),
-            shape((3, 3 * LEV, TILE), F32),
-            shape((3, 3 * LEV, TILE), F32),
-        ],
-        in_specs=[VM] * 3,
-        out_specs=[VM] * 5,
-        scratch_shapes=[
-            pltpu.VMEM((2, 3 * LEV, TILE), F32),
-            pltpu.SemaphoreType.DMA((12,)),
-            pltpu.SemaphoreType.DMA((12,)),
-        ],
-        compiler_params=pltpu.CompilerParams(collective_id=0, has_side_effects=True),
-    )(field, target, mask)
-    final, grads = pl.pallas_call(
-        functools.partial(compute_kernel, sizes),
-        name="local",
-        out_shape=[shape(field.shape, F32), shape((chunk * n_gy, 4 * C), F32)],
-        in_specs=[VM] * 8,
+    dma = pltpu.SemaphoreType.DMA
+    final, summed = pl.pallas_call(
+        functools.partial(fused_kernel, sizes),
+        name="fused",
+        out_shape=[shape(field.shape, F32), shape((n_gy, chunk, 4 * C), BF16)],
+        in_specs=[ANY] * 6,
         out_specs=[VM] * 2,
         scratch_shapes=[
             pltpu.VMEM((3, rows, LEV, wide), F32),
@@ -515,33 +507,40 @@
             pltpu.VMEM((2, h + 2, C, wide), BF16),
             pltpu.VMEM((rows, 3, LEV, wide), F32),
             pltpu.VMEM((2, h, K, width), BF16),
-        ],
-        compiler_params=pltpu.CompilerParams(vmem_limit_bytes=LIMIT),
-    )(own, goal, wet, left, right, conv_one, conv_two, head)
-    dma = pltpu.SemaphoreType.DMA
-    summed = pl.pallas_call(
-        functools.partial(sum_kernel, sizes),
-        name="gradsum",
-        out_shape=shape(grads.shape, F32),
-        in_specs=[VM],
-        out_specs=VM,
-        scratch_shapes=[
+            pltpu.VMEM(field.shape, F32),
+            pltpu.VMEM(target.shape, F32),
+            pltpu.VMEM(mask.shape, jnp.int32),
+            pltpu.VMEM(conv_one.shape, F32),
+            pltpu.VMEM(conv_two.shape, F32),
+            pltpu.VMEM(head.shape, F32),
+            pltpu.VMEM((3, h, width), F32),
+            pltpu.VMEM((3, 3 * LEV, TILE), F32),
+            pltpu.VMEM((3, 3 * LEV, TILE), F32),
+            pltpu.VMEM((2, 3 * LEV, TILE), F32),
+            pltpu.VMEM((n_gy, chunk, 4 * C), F32),
             pltpu.VMEM((n_gy - 1, chunk, 4 * C), F32),
             pltpu.VMEM((chunk, 4 * C), F32),
             pltpu.VMEM((n_gx, chunk, 4 * C), F32),
+            pltpu.VMEM((chunk, 4 * C), BF16),
+            dma((6,)), dma((12,)), dma((12,)),
             dma((n_gy - 1,)), dma((n_gy - 1,)),
             dma((n_gx - 1,)), dma((n_gx - 1,)),
             dma((n_gy - 1,)), dma((n_gy - 1,)),
         ],
-        compiler_params=pltpu.CompilerParams(collective_id=1, has_side_effects=True),
-    )(grads)
-    u1, u2, u3 = pl.pallas_call(
+        compiler_params=pltpu.CompilerParams(
+            collective_id=0, has_side_effects=True, vmem_limit_bytes=LIMIT
+        ),
+    )(field, target, mask, conv_one, conv_two, head)
+    final, u1, u2, u3 = pl.pallas_call(
         finish_kernel,
         name="update",
-        out_shape=[shape(conv_one.shape, F32), shape(conv_two.shape, F32), shape(head.shape, F32)],
-        in_specs=[VM] * 5,
-        out_specs=[VM] * 3,
-    )(summed, d1, d2, d3, ids.reshape(1, -1))
+        out_shape=[
+            shape(field.shape, F32),
+            shape(conv_one.shape, F32), shape(conv_two.shape, F32), shape(head.shape, F32),
+        ],
+        in_specs=[VM] * 6,
+        out_specs=[VM] * 4,
+    )(summed, final, d1, d2, d3, ids.reshape(1, -1))
     return final, u1, u2, u3
 
 

time: 49.5 us -> 42.7 us (0.86)
  Pallas kernels: 48.6 us -> 41.9 us
    pallas_call x4 -> x2, Pallas kernels: 48.6 us -> 41.9 us  [the longest x1 39.8 us: per_device(): pl.pallas_call(functools.partial(fused_kernel, sizes), name='fused', out_...]
where the time goes in v1:
time: 42.7 us; the launch traced here: 42.5 us
  Pallas kernels  41.9 us (98%)
  between operations  0.64 us (1%)
    pallas_call x1, Pallas kernels, per_device(): pl.pallas_call(functools.partial(fused_kernel, sizes), name='fused', out_...  39.8 us
    pallas_call x1, Pallas kernels, per_device(): pl.pallas_call(finish_kernel, name='update', out_shape=[shape(field.shape...  2.14 us

profile of v1, /device:TPU:0, one launch (start us, length us, event | category | flops | bytes accessed | tf_op | source)
XLA Modules:
  0.0 42.5 jit_solution(814897279397026652)
XLA Ops:
  0.6 39.8 %fused.1 = (f32[8,8,256]{2,1,0:T(8,128)}, bf16[8,24,256]{2,1,0:T(8,128)(2,1)}) custom-call(f32[8,8,256]{2,1,0:T(8,128)} %field_in.1, f32[8,8,256]{2,1,0:T(8,128)} %target_in.1, s32[8,256]{1,0:T(8,128)} %mask_in.1, f32[64,73]{1,0:T(8,128)} %w1_in.1, f32[64,577]{1,0:T(8,128)} %w2_in.1, f32[32,65]{1,0:T(8,128)} %w3_in.1), custom_call_target="tpu_custom_call" | custom-call | tf_op jit(solution)/shard_map/fused/pallas_call | solution.py:488
  40.4 2.1 %update.1 = (f32[8,8,256]{2,1,0:T(8,128)}, f32[64,73]{1,0:T(8,128)}, f32[64,577]{1,0:T(8,128)}, f32[32,65]{1,0:T(8,128)}) custom-call(bf16[8,24,256]{2,1,0:T(8,128)(2,1)} %get-tuple-element.6.grads, f32[8,8,256]{2,1,0:T(8,128)} %get-tuple-element.7.final, f32[64,73]{1,0:T(8,128)} %d1.1, f32[64,577]{1,0:T(8,128)} %d2.1, f32[32,65]{1,0:T(8,128)} %d3.1, ...), custom_call_target="tpu_custom_call" | custom-call | tf_op jit(solution)/shard_map/update/pallas_call | solution.py:534

commit v2 on v1

v2 whole, which is shorter than its diff:
```python
import functools
import math

import jax
import jax.numpy as jnp
from jax import lax
from jax.experimental import pallas as pl
from jax.experimental.pallas import tpu as pltpu
from jax.sharding import PartitionSpec as P

GROUPS = 6
PARAMS = 43680
RIM = 6
NEAR = 2
LEV = 8
C = 64
K = 32
TILE = 128
SLOTS = 4
SLOT = TILE // SLOTS
MESH = pl.DeviceIdType.MESH
F32 = jnp.float32
BF16 = jnp.bfloat16
VM = pl.BlockSpec(memory_space=pltpu.VMEM)
ANY = pl.BlockSpec(memory_space=pl.ANY)
LIMIT = 56 * 1024 * 1024
NT = (((1,), (1,)), ((), ()))


def dot(a, b):
    return jnp.dot(a, b, preferred_element_type=F32)


def dot_nt(a, b):
    return lax.dot_general(a, b, NT, preferred_element_type=F32)


def sigmoid(v):
    return 0.5 * jnp.tanh(0.5 * v) + 0.5


def roll(v, shift):
    return pltpu.roll(v, shift % v.shape[1], 1)


def fused_kernel(
    sizes, field_in, target_in, mask_in, w1_in, w2_in, w3_in,
    final_ref, out_ref, rest_ref,
    fo, fh, fl, fr, flh, frh, wo, wh, to, th, ao, ah, ad,
    xo, xh, ho, hh, p1o, p1h, p2o, p2h, t3o, t3h, h2o, eo, eh, e3o, e1o, e1h, vo,
    field, target, mask, w1_ref, w2_ref, w3_ref, wet, left, right, packed,
    grads_ref, got, part, parts, mine, extra_ref, extra_got, extra_part, extra_parts, extra_mine,
    load_sem, send_sem, recv_sem, send_one, recv_one, send_two, recv_two, send_three, recv_three,
    send_four, recv_four, send_five, recv_five, send_six, recv_six,
):
    n_gx, n_gy = sizes
    gx = lax.axis_index("gx")
    gy = lax.axis_index("gy")
    h, width = mask.shape
    rows = h + 2 * RIM
    tiles = rows // SLOTS
    ys = [lax.rem(gy + k, n_gy) for k in range(1, n_gy)]
    xs = [lax.rem(gx + k, n_gx) for k in range(1, n_gx)]
    moves = [(dx, dy) for dx in (-1, 0, 1) for dy in (-1, 0, 1) if (dx, dy) != (0, 0)]

    def exists(dx, dy):
        x = gx + dx
        y = gy + dy
        return (x >= 0) & (x < n_gx) & (y >= 0) & (y < n_gy)

    barrier = pltpu.get_barrier_semaphore()
    count = jnp.int32(n_gy + n_gx - 2)
    for dx, dy in moves:
        if dx and dy:
            @pl.when(exists(dx, dy))
            def _():
                pl.semaphore_signal(barrier, inc=1, device_id=(gx + dx, gy + dy), device_id_type=MESH)
            count = count + jnp.where(exists(dx, dy), 1, 0)
    for x in xs:
        pl.semaphore_signal(barrier, inc=1, device_id=(x, gy), device_id_type=MESH)
    for y in ys:
        pl.semaphore_signal(barrier, inc=1, device_id=(gx, y), device_id_type=MESH)

    loads = [
        pltpu.make_async_copy(src, dst, load_sem.at[i])
        for i, (src, dst) in enumerate(
            [(field_in, field), (target_in, target), (mask_in, mask),
             (w1_in, w1_ref), (w2_in, w2_ref), (w3_in, w3_ref)]
        )
    ]
    for copy in loads:
        copy.start()

    def pairs(dx, dy):
        if dy:
            side = left if dy > 0 else right
            return [(packed.at[0 if dy > 0 else 1], side.at[1 - dx])]
        if dx > 0:
            return [
                (fo.at[0, pl.ds(h, RIM)], fo.at[0, pl.ds(0, RIM)]),
                (to.at[pl.ds(RIM + h - NEAR, NEAR)], to.at[pl.ds(RIM - NEAR, NEAR)]),
                (wet.at[1], wet.at[0]),
            ]
        return [
            (fo.at[0, pl.ds(RIM, RIM)], fo.at[0, pl.ds(RIM + h, RIM)]),
            (to.at[pl.ds(RIM, NEAR)], to.at[pl.ds(RIM + h, NEAR)]),
            (wet.at[1], wet.at[2]),
        ]

    for dx, dy in moves:
        @pl.when(jnp.logical_not(exists(-dx, -dy)))
        def _():
            for _, dst in pairs(dx, dy):
                dst[...] = jnp.zeros(dst.shape, F32)

    for copy in loads[:3]:
        copy.wait()
    lane = lax.broadcasted_iota(jnp.int32, (3 * LEV, TILE), 1)
    strips = [jnp.zeros((3 * LEV, TILE), F32) for _ in range(2)]
    for r in range(h):
        wide_wet = jnp.broadcast_to(mask[r : r + 1, :].astype(F32), (LEV, width))
        values = wide_wet * field[:, r, :]
        goal = target[:, r, :]
        fo[0, RIM + r] = values
        to[RIM + r] = goal
        mixed = jnp.concatenate([values, wide_wet, goal], axis=0)
        here = (lane >= LEV * r) & (lane < LEV * r + LEV)
        low = mixed[:, :TILE]
        high = mixed[:, width - TILE :]
        strips[0] = jnp.where(here, roll(high, LEV * r + LEV), strips[0])
        strips[1] = jnp.where(here, roll(low, LEV * r), strips[1])
    wet[1] = mask[...].astype(F32)
    packed[0] = strips[0]
    packed[1] = strips[1]

    pl.semaphore_wait(barrier, count)

    copies = []
    index = 0
    for dx, dy in moves:
        group = []
        for src, dst in pairs(dx, dy):
            group.append(
                pltpu.make_async_remote_copy(
                    src_ref=src,
                    dst_ref=dst,
                    send_sem=send_sem.at[index],
                    recv_sem=recv_sem.at[index],
                    device_id=(gx + dx, gy + dy),
                    device_id_type=MESH,
                )
            )
            index += 1
        copies.append((dx, dy, group))
    for dx, dy, group in copies:
        @pl.when(exists(dx, dy))
        def _():
            for copy in group:
                copy.start()

    for copy in loads[3:]:
        copy.wait()
    slot_lane = lax.broadcasted_iota(jnp.int32, (1, TILE), 1) % SLOT
    slot_row = lax.broadcasted_iota(jnp.int32, (1, TILE), 1) // SLOT * tiles
    lane1 = lax.broadcasted_iota(jnp.int32, (1, TILE), 1)

    def pad16(v, n):
        return jnp.concatenate([v, jnp.zeros((v.shape[0], n - v.shape[1]), F32)], axis=1)

    def thirds(b):
        high = b.astype(BF16).astype(F32)
        low = b - high
        middle = low.astype(BF16).astype(F32)
        return jnp.concatenate([high, middle, low - middle], axis=1)

    wa = 0.5 * w1_ref[...]
    wb = 0.5 * w2_ref[...]
    wc = 0.5 * w3_ref[...]
    none = jnp.zeros((C, LEV), F32)
    w1 = jnp.concatenate(
        [
            wa[:, : 3 * LEV], none,
            wa[:, 3 * LEV : 6 * LEV], pad16(thirds(wa[:, 9 * LEV :]), LEV),
            wa[:, 6 * LEV : 9 * LEV], none,
        ],
        axis=1,
    ).astype(BF16)
    w2 = jnp.concatenate([wb[:, : 9 * C], pad16(thirds(wb[:, 9 * C :]), 16)], axis=1).astype(BF16)
    w3 = jnp.concatenate([wc[:, :C], pad16(thirds(wc[:, C:]), 16)], axis=1).astype(BF16)
    w3t = wc[:, :C].T.astype(BF16)
    flip = wb[:, : 9 * C].T
    w2t = jnp.concatenate([flip[k * C : (k + 1) * C] for k in range(8, -1, -1)], axis=1).astype(BF16)
    turn = (2.0 * wa[:, : 9 * LEV]).T
    w1t = jnp.concatenate(
        [
            jnp.concatenate(
                [turn[(3 * a + b) * LEV : (3 * a + b + 1) * LEV] for b in (2, 1, 0)], axis=1
            )
            for a in range(3)
        ],
        axis=0,
    ).astype(BF16)
    ones = jnp.ones((16, width), BF16)
    unit = jnp.ones((LEV, width), F32)

    first_lane = lane1 == 0
    last_lane = lane1 == TILE - 1

    def own_left(own, halo, q):
        r0 = roll(own[:, :TILE], 1)
        r1 = roll(own[:, TILE:], 1)
        rh = roll(halo, 1 - SLOT * (q + 1))
        return jnp.concatenate([jnp.where(first_lane, rh, r0), jnp.where(first_lane, r0, r1)], axis=1)

    def own_right(own, halo, q):
        r0 = roll(own[:, :TILE], -1)
        r1 = roll(own[:, TILE:], -1)
        rh = roll(halo, TILE - 1 - SLOT * q)
        return jnp.concatenate([jnp.where(last_lane, r1, r0), jnp.where(last_lane, rh, r1)], axis=1)

    def halo_left(halo, owns):
        out = roll(halo, 1)
        for q, own in enumerate(owns):
            if own is not None:
                out = jnp.where(lane1 == SLOT * q, roll(own[:, TILE:], 1 + SLOT * q), out)
        return out

    def halo_right(halo, owns):
        out = roll(halo, -1)
        for q, own in enumerate(owns):
            if own is not None:
                out = jnp.where(lane1 == SLOT * q + SLOT - 1, roll(own[:, :TILE], SLOT * q + SLOT - 1), out)
        return out

    def at(r):
        return slice(r * width, (r + 1) * width)

    def tile(t, n=1):
        return slice((t + 1) * TILE, (t + 1 + n) * TILE)

    def twist(ref, s):
        ref[s, :, tile(-1)] = roll(ref[s, :, tile(tiles - 1)], SLOT)
        ref[s, :, tile(tiles)] = roll(ref[s, :, tile(0)], -SLOT)

    def stack_own(ref, s, r, *more):
        return jnp.concatenate([ref[s, :, at(r + a)] for a in (-1, 0, 1)] + list(more), axis=0)

    def stack_halo(ref, s, t, n, *more):
        return jnp.concatenate([ref[s, :, tile(t + a, n)] for a in (-1, 0, 1)] + list(more), axis=0)

    pieces = [(t, min(2, tiles - t)) for t in range(0, tiles, 2)]
    up_ok = jnp.where(gx > 0, 1.0, 0.0).astype(F32)
    down_ok = jnp.where(gx < n_gx - 1, 1.0, 0.0).astype(F32)
    left_ok = jnp.where(gy > 0, 1.0, 0.0).astype(F32)
    right_ok = jnp.where(gy < n_gy - 1, 1.0, 0.0).astype(F32)

    def inside_halo(t):
        r = slot_row + t
        side = jnp.where(slot_lane < SLOT // 2, right_ok, left_ok)
        return side * jnp.where(r < RIM, up_ok, jnp.where(r >= RIM + h, down_ok, 1.0))

    def inside_own(v, r):
        return v * up_ok if r < RIM else v * down_ok if r >= RIM + h else v

    in_halo = [inside_halo(t) for t in range(tiles)]

    def halo_mask(t, n):
        return jnp.concatenate(in_halo[t : t + n], axis=1)

    for dx, dy, group in copies:
        @pl.when(exists(-dx, -dy))
        def _():
            for copy in group:
                copy.wait_recv()

    for t in range(tiles):
        side_tile = jnp.zeros((3 * LEV, TILE), F32)
        for q in range(SLOTS):
            r = t + tiles * q
            where = 0 if r < RIM else 1 if r < RIM + h else 2
            k = (r + h - RIM) % h
            is_right = (lane1 >= SLOT * q) & (lane1 < SLOT * q + LEV)
            is_left = (lane1 >= SLOT * q + SLOT - LEV) & (lane1 < SLOT * q + SLOT)
            side_tile = jnp.where(is_right, roll(right[where], SLOT * q - LEV * k), side_tile)
            side_tile = jnp.where(
                is_left, roll(left[where], SLOT * q + SLOT - LEV - LEV * k), side_tile
            )
        fh[0, :, tile(t)] = side_tile[:LEV]
        wh[t] = side_tile[LEV : 2 * LEV]
        th[t] = side_tile[2 * LEV :]
    twist(fh, 0)
    for r in range(rows):
        where = 0 if r < RIM else 1 if r < RIM + h else 2
        k = (r + h - RIM) % h
        wo[r] = jnp.broadcast_to(wet[where, k : k + 1, :], (LEV, width))

    def activate(u):
        t = jnp.tanh(u)
        ut = u * t
        return u + ut, (1.0 + t) * (1.0 + u - ut)

    def forward(s, rad):
        low, high = (0, rows - 1) if s == 0 else (RIM - 4, RIM + h + 3)
        near = lambda r: min(max(r, low), high)
        for t in range(tiles):
            halo = fh[s, :, tile(t)]
            owns = [fo[s, near(t + tiles * q)] for q in range(SLOTS)]
            before = halo_left(halo, owns)
            after = halo_right(halo, owns)
            flh[s, t] = before
            frh[s, t] = after
            xh[s, :, tile(t)] = jnp.concatenate(
                [before, halo, after, unit[:, :TILE]], axis=0
            ).astype(BF16)
        twist(xh, s)
        for r in range(RIM - rad - 2, RIM + h + rad + 2):
            own = fo[s, r]
            halo = fh[s, :, tile(r % tiles)]
            before = own_left(own, halo, r // tiles)
            after = own_right(own, halo, r // tiles)
            fl[s, r] = before
            fr[s, r] = after
            xo[s, :, at(r)] = jnp.concatenate([before, own, after, unit], axis=0).astype(BF16)
        for t, n in pieces:
            hid, slope = activate(dot(w1, stack_halo(xh, s, t, n)))
            ok = halo_mask(t, n)
            p1h[s, :, t * TILE : (t + n) * TILE] = slope * ok
            hh[s, C : 2 * C, tile(t, n)] = (hid * ok).astype(BF16)
        for r in range(RIM - rad - 1, RIM + h + rad + 1):
            hid, slope = activate(dot(w1, stack_own(xo, s, r)))
            if RIM - 1 <= r < RIM + h + 1:
                p1o[s, :, at(r)] = inside_own(slope, r)
            hid = inside_own(hid, r).astype(BF16)
            halo = hh[s, C : 2 * C, tile(r % tiles)]
            ho[s, :, at(r)] = jnp.concatenate(
                [own_left(hid, halo, r // tiles), hid, own_right(hid, halo, r // tiles)], axis=0
            )
        low, high = RIM - rad - 1, RIM + h + rad
        for t in range(tiles):
            halo = hh[s, C : 2 * C, tile(t)]
            owns = [
                ho[s, C : 2 * C, at(t + tiles * q)] if low <= t + tiles * q <= high else None
                for q in range(SLOTS)
            ]
            hh[s, :C, tile(t)] = halo_left(halo, owns)
            hh[s, 2 * C :, tile(t)] = halo_right(halo, owns)
        twist(hh, s)

        def finish(hid, n):
            return jnp.tanh(dot(w3, jnp.concatenate([hid, ones[:, :n]], axis=0)))

        def change(t3, center, others):
            total = 0.0
            for k, other in enumerate(others):
                total = total + (1.0 + t3[k * LEV : (k + 1) * LEV]) * (other - center)
            return total

        for t, n in pieces:
            hid, slope = activate(dot(w2, stack_halo(hh, s, t, n, ones[:, : n * TILE])))
            t3 = finish(hid.astype(BF16), n * TILE)
            if s == 1:
                p2h[:, t * TILE : (t + n) * TILE] = slope
                t3h[:, t * TILE : (t + n) * TILE] = t3
            for i in range(n):
                center = fh[s, :, tile(t + i)]
                fh[s + 1, :, tile(t + i)] = center + 0.125 * wh[t + i] * change(
                    t3[:, i * TILE : (i + 1) * TILE], center,
                    [fh[s, :, tile(t + i + 1)], fh[s, :, tile(t + i - 1)], frh[s, t + i], flh[s, t + i]],
                )
        twist(fh, s + 1)
        for r in range(RIM - rad, RIM + h + rad):
            hid, slope = activate(dot(w2, stack_own(ho, s, r, ones)))
            hid = hid.astype(BF16)
            mine_row = RIM <= r < RIM + h
            if s == 1 or mine_row:
                p2o[s, :, at(r)] = slope
            if mine_row:
                h2o[s, :, at(r - RIM)] = hid
            t3 = finish(hid, width)
            if s == 1 or mine_row:
                t3o[s, :, at(r)] = t3
            center = fo[s, r]
            fo[s + 1, r] = center + 0.125 * wo[r] * change(
                t3, center, [fo[s, r + 1], fo[s, r - 1], fr[s, r], fl[s, r]]
            )

    forward(0, 4)
    forward(1, 2)
    for r in range(h):
        final_ref[:, r, :] = fo[2, RIM + r]

    fold = lambda v: sum(v[:, k * TILE : (k + 1) * TILE] for k in range(v.shape[1] // TILE))

    for r in range(RIM - 2, RIM + h + 2):
        ao[r] = wo[r] * wo[r] * (fo[2, r] - to[r])
    for t in range(tiles):
        ah[t] = wh[t] * wh[t] * (fh[2, :, tile(t)] - th[t])

    def errors(scaled, t3, slope, center, others):
        e3 = jnp.concatenate([scaled * (other - center) for other in others], axis=0) * (1.0 - t3 * t3)
        e3b = e3.astype(BF16)
        return e3, e3b, dot(w3t, e3b) * slope

    sum3 = jnp.zeros((K, TILE), F32)
    sum2 = jnp.zeros((C, TILE), F32)
    sum1 = jnp.zeros((C, TILE), F32)

    def own_errors(s, r, wg, halo):
        e3, e3b, e2 = errors(
            wg * 0.0625, t3o[s, :, at(r)], p2o[s, :, at(r)], fo[s, r],
            [fo[s, r + 1], fo[s, r - 1], fr[s, r], fl[s, r]],
        )
        e2b = e2.astype(BF16)
        eo[s, :, at(r)] = jnp.concatenate(
            [own_left(e2b, halo, r // tiles), e2b, own_right(e2b, halo, r // tiles)], axis=0
        )
        if RIM <= r < RIM + h:
            e3o[s, :, at(r - RIM)] = e3b
        return e3, e2

    for t in range(tiles):
        lanes = slice(t * TILE, (t + 1) * TILE)
        _, _, e2 = errors(
            ah[t] * 0.0625, t3h[:, lanes], p2h[:, lanes], fh[1, :, tile(t)],
            [fh[1, :, tile(t + 1)], fh[1, :, tile(t - 1)], frh[1, t], flh[1, t]],
        )
        eh[1, C : 2 * C, tile(t)] = e2.astype(BF16)
    for r in range(RIM - 2, RIM + h + 2):
        e3, e2 = own_errors(1, r, ao[r], eh[1, C : 2 * C, tile(r % tiles)])
        if RIM <= r < RIM + h:
            sum3 = sum3 + fold(e3)
            sum2 = sum2 + fold(e2)
    for t in range(tiles):
        halo = eh[1, C : 2 * C, tile(t)]
        owns = [
            eo[1, C : 2 * C, at(t + tiles * q)] if RIM - 2 <= t + tiles * q < RIM + h + 2 else None
            for q in range(SLOTS)
        ]
        eh[1, :C, tile(t)] = halo_left(halo, owns)
        eh[1, 2 * C :, tile(t)] = halo_right(halo, owns)
    twist(eh, 1)
    for t, n in pieces:
        e1 = dot(w2t, stack_halo(eh, 1, t, n)) * p1h[1, :, t * TILE : (t + n) * TILE]
        e1h[:, t * TILE : (t + n) * TILE] = e1.astype(BF16)
    for r in range(RIM - 1, RIM + h + 1):
        e1 = dot(w2t, stack_own(eo, 1, r)) * p1o[1, :, at(r)]
        e1b = e1.astype(BF16)
        if RIM <= r < RIM + h:
            e1o[1, :, at(r)] = e1b
            sum1 = sum1 + fold(e1)
        t = r % tiles
        halo = e1h[:, t * TILE : (t + 1) * TILE]
        vo[r] = dot(
            w1t,
            jnp.concatenate(
                [own_left(e1b, halo, r // tiles), e1b, own_right(e1b, halo, r // tiles)], axis=0
            ),
        )

    def carried(k, r):
        return 0.125 * ao[r] * (1.0 + t3o[1, k * LEV : (k + 1) * LEV, at(r)])

    for r in range(RIM, RIM + h):
        t, q = r % tiles, r // tiles
        lanes = slice(t * TILE, (t + 1) * TILE)
        halo = lambda k: 0.125 * ah[t] * (1.0 + t3h[k * LEV : (k + 1) * LEV, lanes])
        parts_here = [carried(k, r) for k in range(4)]
        raw = wo[r] * (fo[2, r] - to[r])
        ad[r - RIM] = (
            raw
            - (parts_here[0] + parts_here[1] + parts_here[2] + parts_here[3])
            + carried(0, r - 1)
            + carried(1, r + 1)
            + own_left(parts_here[2], halo(2), q)
            + own_right(parts_here[3], halo(3), q)
            + vo[r + 1, :LEV]
            + vo[r, LEV : 2 * LEV]
            + vo[r - 1, 2 * LEV :]
        )

    nothing = jnp.zeros((C, TILE), BF16)
    for r in range(RIM, RIM + h):
        e3, e2 = own_errors(0, r, wo[r] * ad[r - RIM], nothing)
        sum3 = sum3 + fold(e3)
        sum2 = sum2 + fold(e2)

    inner = slice(RIM * width, (RIM + h) * width)

    def shifted(ref, s):
        return jnp.concatenate(
            [ref[s, :, (RIM + a) * width : (RIM + a + h) * width] for a in (-1, 0, 1)], axis=0
        )

    g2 = [
        dot_nt(eo[1, C : 2 * C, inner], ho[1, :, (RIM + a) * width : (RIM + a + h) * width])
        + dot_nt(eo[0, C : 2 * C, inner], ho[0, :, (RIM + a) * width : (RIM + a + h) * width])
        for a in (-1, 0, 1)
    ]
    g3 = dot_nt(e3o[1], h2o[1]) + dot_nt(e3o[0], h2o[0])
    big = jnp.concatenate(g2 + [jnp.concatenate([g3, jnp.zeros((C - K, C), F32)], axis=0)], axis=1)
    chunk = grads_ref.shape[1]

    def spread_rows(ref, v):
        for y in range(n_gy):
            lo = y * chunk
            ref[y] = v[lo : lo + chunk] if lo + chunk <= C else jnp.zeros((chunk, v.shape[1]), F32)

    def to_peers(src, dst, send, recv, peers, key):
        return [
            pltpu.make_async_remote_copy(
                src_ref=src(k, p), dst_ref=dst(k, p), send_sem=send.at[k], recv_sem=recv.at[k],
                device_id=key(p), device_id_type=MESH,
            )
            for k, p in enumerate(peers)
        ]

    def begin(group):
        for copy in group:
            copy.start()
        return group

    along_y = lambda y: (gx, y)
    along_x = lambda x: (x, gy)
    spread_rows(grads_ref, big)
    one = begin(to_peers(
        lambda k, y: grads_ref.at[y], lambda k, y: got.at[k], send_one, recv_one, ys, along_y
    ))

    for t in range(tiles):
        owns = [
            eo[0, C : 2 * C, at(t + tiles * q)] if RIM <= t + tiles * q < RIM + h else None
            for q in range(SLOTS)
        ]
        eh[0, C : 2 * C, tile(t)] = nothing
        eh[0, :C, tile(t)] = halo_left(nothing, owns)
        eh[0, 2 * C :, tile(t)] = halo_right(nothing, owns)
    twist(eh, 0)
    for r in (RIM - 2, RIM - 1, RIM + h, RIM + h + 1):
        eo[0, :, at(r)] = jnp.zeros((3 * C, width), BF16)
    g1 = dot_nt(e1o[1, :, inner], shifted(xo, 1))
    for t, n in pieces:
        e1 = dot(w2t, stack_halo(eh, 0, t, n)) * p1h[0, :, t * TILE : (t + n) * TILE]
        sum1 = sum1 + fold(e1)
        g1 = g1 + dot_nt(e1.astype(BF16), stack_halo(xh, 0, t, n))
    for r in range(RIM - 1, RIM + h + 1):
        e1 = dot(w2t, stack_own(eo, 0, r)) * p1o[0, :, at(r)]
        sum1 = sum1 + fold(e1)
        e1o[0, :, at(r)] = e1.astype(BF16)
    ring = h + 2
    g1 = g1 + dot_nt(
        e1o[0, :, (RIM - 1) * width : (RIM + h + 1) * width],
        jnp.concatenate(
            [xo[0, :, (RIM - 1 + a) * width : (RIM - 1 + a + ring) * width] for a in (-1, 0, 1)], axis=0
        ),
    )
    total = lambda v: jnp.sum(v, axis=1, keepdims=True)
    tall = lambda v: jnp.concatenate([v, jnp.zeros((C - v.shape[0], 1), F32)], axis=0)
    extra = pad16(
        jnp.concatenate([g1, total(sum1), total(sum2), tall(total(sum3))], axis=1), TILE
    )
    spread_rows(extra_ref, extra)
    four = begin(to_peers(
        lambda k, y: extra_ref.at[y], lambda k, y: extra_got.at[k], send_four, recv_four, ys, along_y
    ))

    def gather_one(group, ref, arrived, here):
        acc = ref[gy]
        for k, copy in enumerate(group):
            copy.wait_recv()
            acc = acc + arrived[k]
        here[...] = acc
        return acc

    def gather_two(group, ref, acc, to_send, out):
        ref[gx] = acc
        for copy in group:
            copy.wait_recv()
        acc = ref[0]
        for x in range(1, n_gx):
            acc = acc + ref[x]
        acc = acc.astype(BF16)
        to_send[...] = acc
        out[gy] = acc

    acc_big = gather_one(one, grads_ref, got, part)
    two = begin(to_peers(
        lambda k, x: part, lambda k, x: parts.at[gx], send_two, recv_two, xs, along_x
    ))
    acc_extra = gather_one(four, extra_ref, extra_got, extra_part)
    five = begin(to_peers(
        lambda k, x: extra_part, lambda k, x: extra_parts.at[gx], send_five, recv_five, xs, along_x
    ))
    gather_two(two, parts, acc_big, mine, out_ref)
    three = begin(to_peers(
        lambda k, y: mine, lambda k, y: out_ref.at[gy], send_three, recv_three, ys, along_y
    ))
    gather_two(five, extra_parts, acc_extra, extra_mine, rest_ref)
    six = begin(to_peers(
        lambda k, y: extra_mine, lambda k, y: rest_ref.at[gy], send_six, recv_six, ys, along_y
    ))
    for copy in three + six:
        copy.wait_recv()
    for dx, dy, group in copies:
        @pl.when(exists(dx, dy))
        def _():
            for copy in group:
                copy.wait_send()
    for copy in one + two + three + four + five + six:
        copy.wait_send()


def finish_kernel(grads, rest, final, d1, d2, d3, ids, final_out, u1, u2, u3):
    final_out[...] = final[...]
    n_parts = C // grads.shape[1]
    big = jnp.concatenate([grads[y].astype(F32) for y in range(n_parts)], axis=0)
    side = jnp.concatenate([rest[y].astype(F32) for y in range(n_parts)], axis=0)
    one = jnp.concatenate(
        [side[:, 4 * LEV * a : 4 * LEV * a + 3 * LEV] for a in range(3)]
        + [side[:, 12 * LEV : 12 * LEV + 1]],
        axis=1,
    )
    two = jnp.concatenate([big[:, : 9 * C], side[:, 12 * LEV + 1 : 12 * LEV + 2]], axis=1)
    three = jnp.concatenate(
        [big[:K, 9 * C : 10 * C], side[:K, 12 * LEV + 2 : 12 * LEV + 3]], axis=1
    )
    members = [one, two, three]
    heads = [d1[...], d2[...], d3[...]]
    row_sq = lambda v: jnp.sum(v * v, axis=1, keepdims=True)
    grad_rows = jnp.concatenate([row_sq(m) for m in members], axis=0)
    dir_rows = jnp.concatenate([row_sq(m) for m in heads], axis=0)
    total = jnp.sum(grad_rows, axis=0, keepdims=True)
    factor = 1.0 / jnp.maximum(jnp.sqrt(total), 1.0)
    clip_rows = grad_rows * (factor * factor)
    count = grad_rows.shape[0]
    i0 = lax.broadcasted_iota(jnp.int32, (count, count), 0)
    i1 = lax.broadcasted_iota(jnp.int32, (count, count), 1)
    spread = jnp.broadcast_to(ids[...].astype(F32), (count, count))
    column = jnp.sum(jnp.where(i0 == i1, spread, 0.0), axis=1, keepdims=True)
    row_ratio = jnp.zeros((count, 1), F32)
    for k in range(GROUPS):
        hit = column == float(k)
        pick = lambda v: jnp.sum(jnp.where(hit, v, 0.0), axis=0, keepdims=True)
        ratio = jnp.sqrt(pick(clip_rows)) / jnp.sqrt(pick(dir_rows) + 1e-06)
        row_ratio = row_ratio + jnp.where(hit, ratio, 0.0)
    scaling = math.sqrt(PARAMS)
    start = 0
    for ref, member, head in zip((u1, u2, u3), members, heads):
        n = member.shape[0]
        ref[...] = scaling * (member * factor + row_ratio[start : start + n] * head)
        start += n


def per_device(sizes, field, target, mask, conv_one, conv_two, head, d1, d2, d3, ids):
    n_gx, n_gy = sizes
    _, h, width = field.shape
    rows = h + 2 * RIM
    tiles = rows // SLOTS
    flat = rows * width
    edge = (tiles + 2) * TILE
    shape = jax.ShapeDtypeStruct
    chunk = 8 * -(-C // (8 * n_gy))
    wide = 10 * C
    dma = pltpu.SemaphoreType.DMA
    vmem = pltpu.VMEM
    over_y = [dma((n_gy - 1,)), dma((n_gy - 1,))]
    over_x = [dma((n_gx - 1,)), dma((n_gx - 1,))]

    def sums(columns):
        return [
            vmem((n_gy, chunk, columns), F32),
            vmem((n_gy - 1, chunk, columns), F32),
            vmem((chunk, columns), F32),
            vmem((n_gx, chunk, columns), F32),
            vmem((chunk, columns), BF16),
        ]

    final, summed, rest = pl.pallas_call(
        functools.partial(fused_kernel, sizes),
        name="fused",
        out_shape=[
            shape(field.shape, F32),
            shape((n_gy, chunk, wide), BF16),
            shape((n_gy, chunk, TILE), BF16),
        ],
        in_specs=[ANY] * 6,
        out_specs=[VM] * 3,
        scratch_shapes=[
            vmem((3, rows, LEV, width), F32),
            vmem((3, LEV, edge), F32),
            vmem((2, rows, LEV, width), F32),
            vmem((2, rows, LEV, width), F32),
            vmem((2, tiles, LEV, TILE), F32),
            vmem((2, tiles, LEV, TILE), F32),
            vmem((rows, LEV, width), F32),
            vmem((tiles, LEV, TILE), F32),
            vmem((rows, LEV, width), F32),
            vmem((tiles, LEV, TILE), F32),
            vmem((rows, LEV, width), F32),
            vmem((tiles, LEV, TILE), F32),
            vmem((h, LEV, width), F32),
            vmem((2, 4 * LEV, flat), BF16),
            vmem((2, 4 * LEV, edge), BF16),
            vmem((2, 3 * C, flat), BF16),
            vmem((2, 3 * C, edge), BF16),
            vmem((2, C, flat), F32),
            vmem((2, C, tiles * TILE), F32),
            vmem((2, C, flat), F32),
            vmem((C, tiles * TILE), F32),
            vmem((2, K, flat), F32),
            vmem((K, tiles * TILE), F32),
            vmem((2, C, h * width), BF16),
            vmem((2, 3 * C, flat), BF16),
            vmem((2, 3 * C, edge), BF16),
            vmem((2, K, h * width), BF16),
            vmem((2, C, flat), BF16),
            vmem((C, tiles * TILE), BF16),
            vmem((rows, 3 * LEV, width), F32),
            vmem(field.shape, F32),
            vmem(target.shape, F32),
            vmem(mask.shape, jnp.int32),
            vmem(conv_one.shape, F32),
            vmem(conv_two.shape, F32),
            vmem(head.shape, F32),
            vmem((3, h, width), F32),
            vmem((3, 3 * LEV, TILE), F32),
            vmem((3, 3 * LEV, TILE), F32),
            vmem((2, 3 * LEV, TILE), F32),
        ]
        + sums(wide)
        + sums(TILE)
        + [dma((6,)), dma((12,)), dma((12,))]
        + over_y + over_x + over_y
        + over_y + over_x + over_y,
        compiler_params=pltpu.CompilerParams(
            collective_id=0, has_side_effects=True, vmem_limit_bytes=LIMIT
        ),
    )(field, target, mask, conv_one, conv_two, head)
    final, u1, u2, u3 = pl.pallas_call(
        finish_kernel,
        name="update",
        out_shape=[
            shape(field.shape, F32),
            shape(conv_one.shape, F32), shape(conv_two.shape, F32), shape(head.shape, F32),
        ],
        in_specs=[VM] * 7,
        out_specs=[VM] * 4,
    )(summed, rest, final, d1, d2, d3, ids.reshape(1, -1))
    return final, u1, u2, u3


def solution(mesh):
    grid = P(None, "gx", "gy")
    placed = (grid, grid, P("gx", "gy")) + (P(),) * 7
    return jax.shard_map(
        functools.partial(per_device, (mesh.shape["gx"], mesh.shape["gy"])),
        mesh=mesh,
        in_specs=placed,
        out_specs=(grid, P(), P(), P()),
        check_vma=False,
    )
```

time: 42.7 us -> 39.9 us (0.934)
  Pallas kernels: 41.9 us -> 39.1 us
    pallas_call x1, Pallas kernels: 39.8 us -> 36.9 us  [per_device(): pl.pallas_call(functools.partial(fused_kernel, sizes), name='fused', out_...]
where the time goes in v2:
time: 39.9 us; the launch traced here: 39.7 us
  Pallas kernels  39.1 us (98%)
  between operations  0.64 us (2%)
    pallas_call x1, Pallas kernels, per_device(): pl.pallas_call(functools.partial(fused_kernel, sizes), name='fused', out_...  36.9 us
    pallas_call x1, Pallas kernels, per_device(): pl.pallas_call(finish_kernel, name='update', out_shape=[shape(field.shape...  2.17 us

profile of v2, /device:TPU:0, one launch (start us, length us, event | category | flops | bytes accessed | tf_op | source)
XLA Modules:
  0.0 39.7 jit_solution(5668888942741312267)
XLA Ops:
  0.6 36.9 %fused.1 = (f32[8,8,256]{2,1,0:T(8,128)}, bf16[8,8,640]{2,1,0:T(8,128)(2,1)}, bf16[8,8,128]{2,1,0:T(8,128)(2,1)}) custom-call(f32[8,8,256]{2,1,0:T(8,128)} %field_in.1, f32[8,8,256]{2,1,0:T(8,128)} %target_in.1, s32[8,256]{1,0:T(8,128)} %mask_in.1, f32[64,73]{1,0:T(8,128)} %w1_in.1, f32[64,577]{1,0:T(8,128)} %w2_in.1, f32[32,65]{1,0:T(8,128)} %w3_in.1), custom_call_target="tpu_custom_call" | custom-call | tf_op jit(solution)/shard_map/fused/pallas_call | solution.py:677
  37.5 2.2 %update.1 = (f32[8,8,256]{2,1,0:T(8,128)}, f32[64,73]{1,0:T(8,128)}, f32[64,577]{1,0:T(8,128)}, f32[32,65]{1,0:T(8,128)}) custom-call(bf16[8,8,640]{2,1,0:T(8,128)(2,1)} %get-tuple-element.7.grads, bf16[8,8,128]{2,1,0:T(8,128)(2,1)} %get-tuple-element.8.rest, f32[8,8,256]{2,1,0:T(8,128)} %get-tuple-element.9.final, f32[64,73]{1,0:T(8,128)} %d1.1, ...), custom_call_target="tpu_custom_call" | custom-call | tf_op jit(solution)/shard_map/update/pallas_call | solution.py:738

commit v3 on v2

--- a/solution.py
+++ b/solution.py
@@ -47,7 +47,7 @@
     sizes, field_in, target_in, mask_in, w1_in, w2_in, w3_in,
     final_ref, out_ref, rest_ref,
     fo, fh, fl, fr, flh, frh, wo, wh, to, th, ao, ah, ad,
-    xo, xh, ho, hh, p1o, p1h, p2o, p2h, t3o, t3h, h2o, eo, eh, e3o, e1o, e1h, vo,
+    xo, xh, ho, hh, p1o, p1h, p2o, p2h, t3o, t3h, h2o, eo, eh, e3o, e1o, e1h, vo, acc2, acc1, acc3,
     field, target, mask, w1_ref, w2_ref, w3_ref, wet, left, right, packed,
     grads_ref, got, part, parts, mine, extra_ref, extra_got, extra_part, extra_parts, extra_mine,
     load_sem, send_sem, recv_sem, send_one, recv_one, send_two, recv_two, send_three, recv_three,
@@ -160,6 +160,13 @@
 
     for copy in loads[3:]:
         copy.wait()
+    def pipeline(stages, start, stop):
+        last = max(lag for lag, _, _, _ in stages)
+        for i in range(start, stop + last):
+            for lag, low, high, stage in stages:
+                if low <= i - lag < high:
+                    stage(i - lag)
+
     slot_lane = lax.broadcasted_iota(jnp.int32, (1, TILE), 1) % SLOT
     slot_row = lax.broadcasted_iota(jnp.int32, (1, TILE), 1) // SLOT * tiles
     lane1 = lax.broadcasted_iota(jnp.int32, (1, TILE), 1)
@@ -313,7 +320,24 @@
                 [before, halo, after, unit[:, :TILE]], axis=0
             ).astype(BF16)
         twist(xh, s)
-        for r in range(RIM - rad - 2, RIM + h + rad + 2):
+        for t, n in pieces:
+            hid, slope = activate(dot(w1, stack_halo(xh, s, t, n)))
+            ok = halo_mask(t, n)
+            p1h[s, :, t * TILE : (t + n) * TILE] = slope * ok
+            hh[s, C : 2 * C, tile(t, n)] = (hid * ok).astype(BF16)
+        def logits(hid, n):
+            return dot(w3, jnp.concatenate([hid, ones[:, :n]], axis=0))
+
+        def change(t3, center, others):
+            total = 0.0
+            for k, other in enumerate(others):
+                total = total + (1.0 + t3[k * LEV : (k + 1) * LEV]) * (other - center)
+            return total
+
+        first_u, second_u, third_u = {}, {}, {}
+        top, bottom = RIM - rad, RIM + h + rad
+
+        def stack_x(r):
             own = fo[s, r]
             halo = fh[s, :, tile(r % tiles)]
             before = own_left(own, halo, r // tiles)
@@ -321,13 +345,12 @@
             fl[s, r] = before
             fr[s, r] = after
             xo[s, :, at(r)] = jnp.concatenate([before, own, after, unit], axis=0).astype(BF16)
-        for t, n in pieces:
-            hid, slope = activate(dot(w1, stack_halo(xh, s, t, n)))
-            ok = halo_mask(t, n)
-            p1h[s, :, t * TILE : (t + n) * TILE] = slope * ok
-            hh[s, C : 2 * C, tile(t, n)] = (hid * ok).astype(BF16)
-        for r in range(RIM - rad - 1, RIM + h + rad + 1):
-            hid, slope = activate(dot(w1, stack_own(xo, s, r)))
+
+        def dot_first(r):
+            first_u[r] = dot(w1, stack_own(xo, s, r))
+
+        def stack_h(r):
+            hid, slope = activate(first_u.pop(r))
             if RIM - 1 <= r < RIM + h + 1:
                 p1o[s, :, at(r)] = inside_own(slope, r)
             hid = inside_own(hid, r).astype(BF16)
@@ -335,31 +358,68 @@
             ho[s, :, at(r)] = jnp.concatenate(
                 [own_left(hid, halo, r // tiles), hid, own_right(hid, halo, r // tiles)], axis=0
             )
-        low, high = RIM - rad - 1, RIM + h + rad
-        for t in range(tiles):
+
+        def dot_second(r):
+            second_u[r] = dot(w2, stack_own(ho, s, r, ones))
+
+        def dot_third(r):
+            hid, slope = activate(second_u.pop(r))
+            hid = hid.astype(BF16)
+            mine_row = RIM <= r < RIM + h
+            if s == 1 or mine_row:
+                p2o[s, :, at(r)] = slope
+            if mine_row:
+                h2o[s, :, at(r - RIM)] = hid
+            third_u[r] = logits(hid, width)
+
+        def advance(r):
+            t3 = jnp.tanh(third_u.pop(r))
+            if s == 1 or RIM <= r < RIM + h:
+                t3o[s, :, at(r)] = t3
+            center = fo[s, r]
+            fo[s + 1, r] = center + 0.125 * wo[r] * change(
+                t3, center, [fo[s, r + 1], fo[s, r - 1], fr[s, r], fl[s, r]]
+            )
+
+        def halo_h(t):
             halo = hh[s, C : 2 * C, tile(t)]
             owns = [
-                ho[s, C : 2 * C, at(t + tiles * q)] if low <= t + tiles * q <= high else None
+                ho[s, C : 2 * C, at(t + tiles * q)] if top - 1 <= t + tiles * q <= bottom else None
                 for q in range(SLOTS)
             ]
             hh[s, :C, tile(t)] = halo_left(halo, owns)
             hh[s, 2 * C :, tile(t)] = halo_right(halo, owns)
+
+        pipeline(
+            [
+                (0, top - 2, bottom + 2, stack_x),
+                (2, top - 1, bottom + 1, dot_first),
+                (3, top - 1, bottom + 1, stack_h),
+                (5, top, bottom, dot_second),
+                (6, top, bottom, dot_third),
+                (7, top, bottom, advance),
+            ],
+            top - 2, bottom + 2,
+        )
+        for t in range(tiles):
+            halo_h(t)
         twist(hh, s)
 
-        def finish(hid, n):
-            return jnp.tanh(dot(w3, jnp.concatenate([hid, ones[:, :n]], axis=0)))
-
-        def change(t3, center, others):
-            total = 0.0
-            for k, other in enumerate(others):
-                total = total + (1.0 + t3[k * LEV : (k + 1) * LEV]) * (other - center)
-            return total
-
-        for t, n in pieces:
-            hid, slope = activate(dot(w2, stack_halo(hh, s, t, n, ones[:, : n * TILE])))
-            t3 = finish(hid.astype(BF16), n * TILE)
+        def halo_second(i):
+            t, n = pieces[i]
+            second_u[i] = dot(w2, stack_halo(hh, s, t, n, ones[:, : n * TILE]))
+
+        def halo_third(i):
+            t, n = pieces[i]
+            hid, slope = activate(second_u.pop(i))
             if s == 1:
                 p2h[:, t * TILE : (t + n) * TILE] = slope
+            third_u[i] = logits(hid.astype(BF16), n * TILE)
+
+        def halo_advance(i):
+            t, n = pieces[i]
+            t3 = jnp.tanh(third_u.pop(i))
+            if s == 1:
                 t3h[:, t * TILE : (t + n) * TILE] = t3
             for i in range(n):
                 center = fh[s, :, tile(t + i)]
@@ -367,22 +427,13 @@
                     t3[:, i * TILE : (i + 1) * TILE], center,
                     [fh[s, :, tile(t + i + 1)], fh[s, :, tile(t + i - 1)], frh[s, t + i], flh[s, t + i]],
                 )
+
+        count = len(pieces)
+        pipeline(
+            [(0, 0, count, halo_second), (1, 0, count, halo_third), (2, 0, count, halo_advance)],
+            0, count,
+        )
         twist(fh, s + 1)
-        for r in range(RIM - rad, RIM + h + rad):
-            hid, slope = activate(dot(w2, stack_own(ho, s, r, ones)))
-            hid = hid.astype(BF16)
-            mine_row = RIM <= r < RIM + h
-            if s == 1 or mine_row:
-                p2o[s, :, at(r)] = slope
-            if mine_row:
-                h2o[s, :, at(r - RIM)] = hid
-            t3 = finish(hid, width)
-            if s == 1 or mine_row:
-                t3o[s, :, at(r)] = t3
-            center = fo[s, r]
-            fo[s + 1, r] = center + 0.125 * wo[r] * change(
-                t3, center, [fo[s, r + 1], fo[s, r - 1], fr[s, r], fl[s, r]]
-            )
 
     forward(0, 4)
     forward(1, 2)
@@ -392,48 +443,69 @@
     fold = lambda v: sum(v[:, k * TILE : (k + 1) * TILE] for k in range(v.shape[1] // TILE))
 
     for r in range(RIM - 2, RIM + h + 2):
-        ao[r] = wo[r] * wo[r] * (fo[2, r] - to[r])
+        ao[r] = wo[r] * (fo[2, r] - to[r])
     for t in range(tiles):
-        ah[t] = wh[t] * wh[t] * (fh[2, :, tile(t)] - th[t])
-
-    def errors(scaled, t3, slope, center, others):
+        ah[t] = wh[t] * (fh[2, :, tile(t)] - th[t])
+
+    def errors(scaled, t3, center, others):
         e3 = jnp.concatenate([scaled * (other - center) for other in others], axis=0) * (1.0 - t3 * t3)
-        e3b = e3.astype(BF16)
-        return e3, e3b, dot(w3t, e3b) * slope
-
-    sum3 = jnp.zeros((K, TILE), F32)
-    sum2 = jnp.zeros((C, TILE), F32)
-    sum1 = jnp.zeros((C, TILE), F32)
-
-    def own_errors(s, r, wg, halo):
-        e3, e3b, e2 = errors(
-            wg * 0.0625, t3o[s, :, at(r)], p2o[s, :, at(r)], fo[s, r],
-            [fo[s, r + 1], fo[s, r - 1], fr[s, r], fl[s, r]],
+        return e3, e3.astype(BF16)
+
+    sums = {
+        3: jnp.zeros((K, TILE), F32), 2: jnp.zeros((C, TILE), F32), 1: jnp.zeros((C, TILE), F32)
+    }
+    own_rows = range(RIM, RIM + h)
+    back, raw_one = {}, {}
+
+    def dot_errors(s, r):
+        wg = ao[r] if s else wo[r] * ad[r - RIM]
+        e3, e3b = errors(
+            wg * 0.0625, t3o[s, :, at(r)], fo[s, r], [fo[s, r + 1], fo[s, r - 1], fr[s, r], fl[s, r]]
         )
+        back[r] = dot(w3t, e3b)
+        if r in own_rows:
+            e3o[s, :, at(r - RIM)] = e3b
+            sums[3] = sums[3] + fold(e3)
+
+    def stack_errors(s, r, halo):
+        e2 = back.pop(r) * p2o[s, :, at(r)]
         e2b = e2.astype(BF16)
         eo[s, :, at(r)] = jnp.concatenate(
             [own_left(e2b, halo, r // tiles), e2b, own_right(e2b, halo, r // tiles)], axis=0
         )
-        if RIM <= r < RIM + h:
-            e3o[s, :, at(r - RIM)] = e3b
-        return e3, e2
+        if r in own_rows:
+            sums[2] = sums[2] + fold(e2)
+
+    def dot_back(s, r):
+        raw_one[r] = dot(w2t, stack_own(eo, s, r))
+
+    def keep_one(s, r):
+        e1 = raw_one.pop(r) * p1o[s, :, at(r)]
+        e1o[s, :, at(r)] = e1.astype(BF16)
+        if s == 0 or r in own_rows:
+            sums[1] = sums[1] + fold(e1)
 
     for t in range(tiles):
         lanes = slice(t * TILE, (t + 1) * TILE)
-        _, _, e2 = errors(
-            ah[t] * 0.0625, t3h[:, lanes], p2h[:, lanes], fh[1, :, tile(t)],
+        _, e3b = errors(
+            ah[t] * 0.0625, t3h[:, lanes], fh[1, :, tile(t)],
             [fh[1, :, tile(t + 1)], fh[1, :, tile(t - 1)], frh[1, t], flh[1, t]],
         )
-        eh[1, C : 2 * C, tile(t)] = e2.astype(BF16)
-    for r in range(RIM - 2, RIM + h + 2):
-        e3, e2 = own_errors(1, r, ao[r], eh[1, C : 2 * C, tile(r % tiles)])
-        if RIM <= r < RIM + h:
-            sum3 = sum3 + fold(e3)
-            sum2 = sum2 + fold(e2)
+        eh[1, C : 2 * C, tile(t)] = (dot(w3t, e3b) * p2h[:, lanes]).astype(BF16)
+    top, bottom = RIM - 2, RIM + h + 2
+    pipeline(
+        [
+            (0, top, bottom, lambda r: dot_errors(1, r)),
+            (1, top, bottom, lambda r: stack_errors(1, r, eh[1, C : 2 * C, tile(r % tiles)])),
+            (3, top + 1, bottom - 1, lambda r: dot_back(1, r)),
+            (4, top + 1, bottom - 1, lambda r: keep_one(1, r)),
+        ],
+        top, bottom,
+    )
     for t in range(tiles):
         halo = eh[1, C : 2 * C, tile(t)]
         owns = [
-            eo[1, C : 2 * C, at(t + tiles * q)] if RIM - 2 <= t + tiles * q < RIM + h + 2 else None
+            eo[1, C : 2 * C, at(t + tiles * q)] if top <= t + tiles * q < bottom else None
             for q in range(SLOTS)
         ]
         eh[1, :C, tile(t)] = halo_left(halo, owns)
@@ -442,13 +514,20 @@
     for t, n in pieces:
         e1 = dot(w2t, stack_halo(eh, 1, t, n)) * p1h[1, :, t * TILE : (t + n) * TILE]
         e1h[:, t * TILE : (t + n) * TILE] = e1.astype(BF16)
-    for r in range(RIM - 1, RIM + h + 1):
-        e1 = dot(w2t, stack_own(eo, 1, r)) * p1o[1, :, at(r)]
-        e1b = e1.astype(BF16)
-        if RIM <= r < RIM + h:
-            e1o[1, :, at(r)] = e1b
-            sum1 = sum1 + fold(e1)
+
+    inner = slice(RIM * width, (RIM + h) * width)
+
+    def shifted(ref, s):
+        return jnp.concatenate(
+            [ref[s, :, (RIM + a) * width : (RIM + a + h) * width] for a in (-1, 0, 1)], axis=0
+        )
+
+    def grad_two(s, a):
+        return dot_nt(eo[s, C : 2 * C, inner], ho[s, :, (RIM + a) * width : (RIM + a + h) * width])
+
+    def carry_field(r):
         t = r % tiles
+        e1b = e1o[1, :, at(r)]
         halo = e1h[:, t * TILE : (t + 1) * TILE]
         vo[r] = dot(
             w1t,
@@ -460,14 +539,13 @@
     def carried(k, r):
         return 0.125 * ao[r] * (1.0 + t3o[1, k * LEV : (k + 1) * LEV, at(r)])
 
-    for r in range(RIM, RIM + h):
+    def adjoint(r):
         t, q = r % tiles, r // tiles
         lanes = slice(t * TILE, (t + 1) * TILE)
         halo = lambda k: 0.125 * ah[t] * (1.0 + t3h[k * LEV : (k + 1) * LEV, lanes])
         parts_here = [carried(k, r) for k in range(4)]
-        raw = wo[r] * (fo[2, r] - to[r])
         ad[r - RIM] = (
-            raw
+            ao[r]
             - (parts_here[0] + parts_here[1] + parts_here[2] + parts_here[3])
             + carried(0, r - 1)
             + carried(1, r + 1)
@@ -478,25 +556,29 @@
             + vo[r - 1, 2 * LEV :]
         )
 
+    def early(i):
+        if i < 3:
+            acc2[i] = grad_two(1, i - 1)
+        elif i == 3:
+            acc1[...] = dot_nt(e1o[1, :, inner], shifted(xo, 1))
+        else:
+            acc3[...] = dot_nt(e3o[1], h2o[1])
+
     nothing = jnp.zeros((C, TILE), BF16)
-    for r in range(RIM, RIM + h):
-        e3, e2 = own_errors(0, r, wo[r] * ad[r - RIM], nothing)
-        sum3 = sum3 + fold(e3)
-        sum2 = sum2 + fold(e2)
-
-    inner = slice(RIM * width, (RIM + h) * width)
-
-    def shifted(ref, s):
-        return jnp.concatenate(
-            [ref[s, :, (RIM + a) * width : (RIM + a + h) * width] for a in (-1, 0, 1)], axis=0
-        )
-
-    g2 = [
-        dot_nt(eo[1, C : 2 * C, inner], ho[1, :, (RIM + a) * width : (RIM + a + h) * width])
-        + dot_nt(eo[0, C : 2 * C, inner], ho[0, :, (RIM + a) * width : (RIM + a + h) * width])
-        for a in (-1, 0, 1)
-    ]
-    g3 = dot_nt(e3o[1], h2o[1]) + dot_nt(e3o[0], h2o[0])
+    low, high = RIM, RIM + h
+    pipeline(
+        [
+            (0, low - 1, high + 1, carry_field),
+            (2, low, high, adjoint),
+            (3, low, high, lambda r: dot_errors(0, r)),
+            (4, low, high, lambda r: stack_errors(0, r, nothing)),
+            (low, 0, 5, early),
+        ],
+        low - 1, high + 1,
+    )
+
+    g2 = [acc2[a] + grad_two(0, a - 1) for a in range(3)]
+    g3 = acc3[...] + dot_nt(e3o[0], h2o[0])
     big = jnp.concatenate(g2 + [jnp.concatenate([g3, jnp.zeros((C - K, C), F32)], axis=0)], axis=1)
     chunk = grads_ref.shape[1]
 
@@ -537,15 +619,18 @@
     twist(eh, 0)
     for r in (RIM - 2, RIM - 1, RIM + h, RIM + h + 1):
         eo[0, :, at(r)] = jnp.zeros((3 * C, width), BF16)
-    g1 = dot_nt(e1o[1, :, inner], shifted(xo, 1))
+    g1 = acc1[...]
     for t, n in pieces:
         e1 = dot(w2t, stack_halo(eh, 0, t, n)) * p1h[0, :, t * TILE : (t + n) * TILE]
-        sum1 = sum1 + fold(e1)
+        sums[1] = sums[1] + fold(e1)
         g1 = g1 + dot_nt(e1.astype(BF16), stack_halo(xh, 0, t, n))
-    for r in range(RIM - 1, RIM + h + 1):
-        e1 = dot(w2t, stack_own(eo, 0, r)) * p1o[0, :, at(r)]
-        sum1 = sum1 + fold(e1)
-        e1o[0, :, at(r)] = e1.astype(BF16)
+    pipeline(
+        [
+            (0, low - 1, high + 1, lambda r: dot_back(0, r)),
+            (1, low - 1, high + 1, lambda r: keep_one(0, r)),
+        ],
+        low - 1, high + 1,
+    )
     ring = h + 2
     g1 = g1 + dot_nt(
         e1o[0, :, (RIM - 1) * width : (RIM + h + 1) * width],
@@ -556,7 +641,7 @@
     total = lambda v: jnp.sum(v, axis=1, keepdims=True)
     tall = lambda v: jnp.concatenate([v, jnp.zeros((C - v.shape[0], 1), F32)], axis=0)
     extra = pad16(
-        jnp.concatenate([g1, total(sum1), total(sum2), tall(total(sum3))], axis=1), TILE
+        jnp.concatenate([g1, total(sums[1]), total(sums[2]), tall(total(sums[3]))], axis=1), TILE
     )
     spread_rows(extra_ref, extra)
     four = begin(to_peers(
@@ -715,6 +800,9 @@
             vmem((2, C, flat), BF16),
             vmem((C, tiles * TILE), BF16),
             vmem((rows, 3 * LEV, width), F32),
+            vmem((3, C, 3 * C), F32),
+            vmem((C, 12 * LEV), F32),
+            vmem((K, C), F32),
             vmem(field.shape, F32),
             vmem(target.shape, F32),
             vmem(mask.shape, jnp.int32),

time: 39.9 us -> 34.9 us (0.87)
  Pallas kernels: 39.1 us -> 34.1 us
    pallas_call x1, Pallas kernels: 36.9 us -> 31.9 us  [per_device(): pl.pallas_call(functools.partial(fused_kernel, sizes), name='fused', out_...]
where the time goes in v3:
time: 34.9 us; the launch traced here: 34.7 us
  Pallas kernels  34.1 us (98%)
  between operations  0.64 us (2%)
    pallas_call x1, Pallas kernels, per_device(): pl.pallas_call(functools.partial(fused_kernel, sizes), name='fused', out_...  31.9 us
    pallas_call x1, Pallas kernels, per_device(): pl.pallas_call(finish_kernel, name='update', out_shape=[shape(field.shape...  2.17 us

profile of v3, /device:TPU:0, one launch (start us, length us, event | category | flops | bytes accessed | tf_op | source)
XLA Modules:
  0.0 34.7 jit_solution(13828635088650655397)
XLA Ops:
  0.6 31.9 %fused.1 = (f32[8,8,256]{2,1,0:T(8,128)}, bf16[8,8,640]{2,1,0:T(8,128)(2,1)}, bf16[8,8,128]{2,1,0:T(8,128)(2,1)}) custom-call(f32[8,8,256]{2,1,0:T(8,128)} %field_in.1, f32[8,8,256]{2,1,0:T(8,128)} %target_in.1, s32[8,256]{1,0:T(8,128)} %mask_in.1, f32[64,73]{1,0:T(8,128)} %w1_in.1, f32[64,577]{1,0:T(8,128)} %w2_in.1, f32[32,65]{1,0:T(8,128)} %w3_in.1), custom_call_target="tpu_custom_call" | custom-call | tf_op jit(solution)/shard_map/fused/pallas_call | solution.py:762
  32.5 2.2 %update.1 = (f32[8,8,256]{2,1,0:T(8,128)}, f32[64,73]{1,0:T(8,128)}, f32[64,577]{1,0:T(8,128)}, f32[32,65]{1,0:T(8,128)}) custom-call(bf16[8,8,640]{2,1,0:T(8,128)(2,1)} %get-tuple-element.7.grads, bf16[8,8,128]{2,1,0:T(8,128)(2,1)} %get-tuple-element.8.rest, f32[8,8,256]{2,1,0:T(8,128)} %get-tuple-element.9.final, f32[64,73]{1,0:T(8,128)} %d1.1, ...), custom_call_target="tpu_custom_call" | custom-call | tf_op jit(solution)/shard_map/update/pallas_call | solution.py:826

commit v4 on v3

--- a/solution.py
+++ b/solution.py
@@ -45,13 +45,12 @@
 
 def fused_kernel(
     sizes, field_in, target_in, mask_in, w1_in, w2_in, w3_in,
-    final_ref, out_ref, rest_ref,
+    final_ref, out_ref,
     fo, fh, fl, fr, flh, frh, wo, wh, to, th, ao, ah, ad,
     xo, xh, ho, hh, p1o, p1h, p2o, p2h, t3o, t3h, h2o, eo, eh, e3o, e1o, e1h, vo, acc2, acc1, acc3,
-    field, target, mask, w1_ref, w2_ref, w3_ref, wet, left, right, packed,
-    grads_ref, got, part, parts, mine, extra_ref, extra_got, extra_part, extra_parts, extra_mine,
+    field, target, mask, w1_ref, w2_ref, w3_ref, wet, left, right, left_rest, right_rest, packed, packed_rest,
+    grads_ref, got, part, parts, mine,
     load_sem, send_sem, recv_sem, send_one, recv_one, send_two, recv_two, send_three, recv_three,
-    send_four, recv_four, send_five, recv_five, send_six, recv_six,
 ):
     n_gx, n_gy = sizes
     gx = lax.axis_index("gx")
@@ -93,18 +92,23 @@
 
     def pairs(dx, dy):
         if dy:
+            k = 0 if dy > 0 else 1
             side = left if dy > 0 else right
-            return [(packed.at[0 if dy > 0 else 1], side.at[1 - dx])]
+            rest = left_rest if dy > 0 else right_rest
+            return [
+                (packed.at[k], side.at[1 - dx]),
+                (packed_rest.at[k], rest.at[1 - dx]),
+            ]
         if dx > 0:
             return [
                 (fo.at[0, pl.ds(h, RIM)], fo.at[0, pl.ds(0, RIM)]),
+                (wet.at[1], wet.at[0]),
                 (to.at[pl.ds(RIM + h - NEAR, NEAR)], to.at[pl.ds(RIM - NEAR, NEAR)]),
-                (wet.at[1], wet.at[0]),
             ]
         return [
             (fo.at[0, pl.ds(RIM, RIM)], fo.at[0, pl.ds(RIM + h, RIM)]),
+            (wet.at[1], wet.at[2]),
             (to.at[pl.ds(RIM, NEAR)], to.at[pl.ds(RIM + h, NEAR)]),
-            (wet.at[1], wet.at[2]),
         ]
 
     for dx, dy in moves:
@@ -130,8 +134,9 @@
         strips[0] = jnp.where(here, roll(high, LEV * r + LEV), strips[0])
         strips[1] = jnp.where(here, roll(low, LEV * r), strips[1])
     wet[1] = mask[...].astype(F32)
-    packed[0] = strips[0]
-    packed[1] = strips[1]
+    for k in range(2):
+        packed[k] = strips[k][:LEV]
+        packed_rest[k] = strips[k][LEV:]
 
     pl.semaphore_wait(barrier, count)
 
@@ -152,11 +157,12 @@
             )
             index += 1
         copies.append((dx, dy, group))
-    for dx, dy, group in copies:
-        @pl.when(exists(dx, dy))
-        def _():
-            for copy in group:
-                copy.start()
+    for part_of in (slice(0, 1), slice(1, None)):
+        for dx, dy, group in copies:
+            @pl.when(exists(dx, dy))
+            def _():
+                for copy in group[part_of]:
+                    copy.start()
 
     for copy in loads[3:]:
         copy.wait()
@@ -216,28 +222,33 @@
     def own_left(own, halo, q):
         r0 = roll(own[:, :TILE], 1)
         r1 = roll(own[:, TILE:], 1)
-        rh = roll(halo, 1 - SLOT * (q + 1))
+        rh = roll(halo, 1 + LEV - SLOT * (q + 1))
         return jnp.concatenate([jnp.where(first_lane, rh, r0), jnp.where(first_lane, r0, r1)], axis=1)
 
     def own_right(own, halo, q):
         r0 = roll(own[:, :TILE], -1)
         r1 = roll(own[:, TILE:], -1)
-        rh = roll(halo, TILE - 1 - SLOT * q)
+        rh = roll(halo, TILE - 1 - LEV - SLOT * q)
         return jnp.concatenate([jnp.where(last_lane, r1, r0), jnp.where(last_lane, rh, r1)], axis=1)
 
-    def halo_left(halo, owns):
-        out = roll(halo, 1)
+    def edge_left(owns):
+        out = jnp.zeros((C, TILE), BF16)
         for q, own in enumerate(owns):
             if own is not None:
-                out = jnp.where(lane1 == SLOT * q, roll(own[:, TILE:], 1 + SLOT * q), out)
+                lane = SLOT * q + LEV
+                out = jnp.where(lane1 == lane, roll(own[:, TILE:], lane + 1), out)
         return out
 
-    def halo_right(halo, owns):
-        out = roll(halo, -1)
+    def edge_right(owns):
+        out = jnp.zeros((C, TILE), BF16)
         for q, own in enumerate(owns):
             if own is not None:
-                out = jnp.where(lane1 == SLOT * q + SLOT - 1, roll(own[:, :TILE], SLOT * q + SLOT - 1), out)
+                lane = SLOT * (q + 1) - LEV - 1
+                out = jnp.where(lane1 == lane, roll(own[:, :TILE], lane), out)
         return out
+
+    def around(v):
+        return roll(v, 1), v, roll(v, -1)
 
     def at(r):
         return slice(r * width, (r + 1) * width)
@@ -264,6 +275,7 @@
     def inside_halo(t):
         r = slot_row + t
         side = jnp.where(slot_lane < SLOT // 2, right_ok, left_ok)
+        side = jnp.where((slot_lane < LEV) | (slot_lane >= SLOT - LEV), 1.0, side)
         return side * jnp.where(r < RIM, up_ok, jnp.where(r >= RIM + h, down_ok, 1.0))
 
     def inside_own(v, r):
@@ -274,66 +286,123 @@
     def halo_mask(t, n):
         return jnp.concatenate(in_halo[t : t + n], axis=1)
 
-    for dx, dy, group in copies:
-        @pl.when(exists(-dx, -dy))
-        def _():
-            for copy in group:
-                copy.wait_recv()
-
-    for t in range(tiles):
-        side_tile = jnp.zeros((3 * LEV, TILE), F32)
+    def arrive(part_of):
+        for dx, dy, group in copies:
+            @pl.when(exists(-dx, -dy))
+            def _():
+                for copy in group[part_of]:
+                    copy.wait_recv()
+
+    def place(r):
+        return (0 if r < RIM else 1 if r < RIM + h else 2), (r + h - RIM) % h
+
+    def side_tile(t, from_right, from_left, own):
+        out = None
         for q in range(SLOTS):
-            r = t + tiles * q
-            where = 0 if r < RIM else 1 if r < RIM + h else 2
-            k = (r + h - RIM) % h
-            is_right = (lane1 >= SLOT * q) & (lane1 < SLOT * q + LEV)
-            is_left = (lane1 >= SLOT * q + SLOT - LEV) & (lane1 < SLOT * q + SLOT)
-            side_tile = jnp.where(is_right, roll(right[where], SLOT * q - LEV * k), side_tile)
-            side_tile = jnp.where(
-                is_left, roll(left[where], SLOT * q + SLOT - LEV - LEV * k), side_tile
-            )
-        fh[0, :, tile(t)] = side_tile[:LEV]
-        wh[t] = side_tile[LEV : 2 * LEV]
-        th[t] = side_tile[2 * LEV :]
-    twist(fh, 0)
-    for r in range(rows):
-        where = 0 if r < RIM else 1 if r < RIM + h else 2
-        k = (r + h - RIM) % h
-        wo[r] = jnp.broadcast_to(wet[where, k : k + 1, :], (LEV, width))
+            where, k = place(t + tiles * q)
+            row = own(t + tiles * q)
+            base = SLOT * q
+            for lane, piece, shift in (
+                (base, row[:, TILE:], base + LEV),
+                (base + LEV, from_right[where], base + LEV - LEV * k),
+                (base + 2 * LEV, from_left[where], base + 2 * LEV - LEV * k),
+                (base + 3 * LEV, row[:, :TILE], base + 3 * LEV),
+            ):
+                moved = roll(piece, shift)
+                out = moved if out is None else jnp.where(lane1 >= lane, moved, out)
+        return out
+
+    def widen(r):
+        where, k = place(r)
+        return jnp.broadcast_to(wet[where, k : k + 1, :], (LEV, width))
+
+    def aim(r):
+        inner_row = RIM - NEAR <= r < RIM + h + NEAR
+        return to[r] if inner_row else jnp.zeros((LEV, width), F32)
 
     def activate(u):
         t = jnp.tanh(u)
         ut = u * t
         return u + ut, (1.0 + t) * (1.0 + u - ut)
 
-    def forward(s, rad):
-        low, high = (0, rows - 1) if s == 0 else (RIM - 4, RIM + h + 3)
-        near = lambda r: min(max(r, low), high)
-        for t in range(tiles):
-            halo = fh[s, :, tile(t)]
-            owns = [fo[s, near(t + tiles * q)] for q in range(SLOTS)]
-            before = halo_left(halo, owns)
-            after = halo_right(halo, owns)
+    def logits(hid, n):
+        return dot(w3, jnp.concatenate([hid, ones[:, :n]], axis=0))
+
+    def change(t3, center, others):
+        total = 0.0
+        for k, other in enumerate(others):
+            total = total + (1.0 + t3[k * LEV : (k + 1) * LEV]) * (other - center)
+        return total
+
+    count = len(pieces)
+
+    def halo_input(s):
+        def stack_x(t):
+            before, halo, after = around(fh[s, :, tile(t)])
             flh[s, t] = before
             frh[s, t] = after
             xh[s, :, tile(t)] = jnp.concatenate(
                 [before, halo, after, unit[:, :TILE]], axis=0
             ).astype(BF16)
-        twist(xh, s)
-        for t, n in pieces:
+
+        def all_x():
+            for t in range(tiles):
+                stack_x(t)
+            twist(xh, s)
+
+        def first(i):
+            t, n = pieces[i]
             hid, slope = activate(dot(w1, stack_halo(xh, s, t, n)))
             ok = halo_mask(t, n)
             p1h[s, :, t * TILE : (t + n) * TILE] = slope * ok
-            hh[s, C : 2 * C, tile(t, n)] = (hid * ok).astype(BF16)
-        def logits(hid, n):
-            return dot(w3, jnp.concatenate([hid, ones[:, :n]], axis=0))
-
-        def change(t3, center, others):
-            total = 0.0
-            for k, other in enumerate(others):
-                total = total + (1.0 + t3[k * LEV : (k + 1) * LEV]) * (other - center)
-            return total
-
+            hid = (hid * ok).astype(BF16)
+            for j in range(n):
+                hh[s, :, tile(t + j)] = jnp.concatenate(
+                    around(hid[:, j * TILE : (j + 1) * TILE]), axis=0
+                )
+
+        return (
+            [all_x]
+            + [functools.partial(first, i) for i in range(count)]
+            + [lambda: twist(hh, s)]
+        )
+
+    def halo_step(s):
+        second_u, third_u = {}, {}
+
+        def second(i):
+            t, n = pieces[i]
+            second_u[i] = dot(w2, stack_halo(hh, s, t, n, ones[:, : n * TILE]))
+
+        def third(i):
+            t, n = pieces[i]
+            hid, slope = activate(second_u.pop(i))
+            if s == 1:
+                p2h[:, t * TILE : (t + n) * TILE] = slope
+            third_u[i] = logits(hid.astype(BF16), n * TILE)
+
+        def advance(i):
+            t, n = pieces[i]
+            t3 = jnp.tanh(third_u.pop(i))
+            if s == 1:
+                t3h[:, t * TILE : (t + n) * TILE] = t3
+            for j in range(n):
+                center = fh[s, :, tile(t + j)]
+                fh[s + 1, :, tile(t + j)] = center + 0.125 * wh[t + j] * change(
+                    t3[:, j * TILE : (j + 1) * TILE], center,
+                    [fh[s, :, tile(t + j + 1)], fh[s, :, tile(t + j - 1)], frh[s, t + j], flh[s, t + j]],
+                )
+
+        order = []
+        for i in range(count + 2):
+            order += [
+                functools.partial(stage, i - lag)
+                for lag, stage in ((0, second), (1, third), (2, advance))
+                if 0 <= i - lag < count
+            ]
+        return order + [lambda: twist(fh, s + 1)]
+
+    def forward(s, rad, beside):
         first_u, second_u, third_u = {}, {}, {}
         top, bottom = RIM - rad, RIM + h + rad
 
@@ -381,15 +450,6 @@
                 t3, center, [fo[s, r + 1], fo[s, r - 1], fr[s, r], fl[s, r]]
             )
 
-        def halo_h(t):
-            halo = hh[s, C : 2 * C, tile(t)]
-            owns = [
-                ho[s, C : 2 * C, at(t + tiles * q)] if top - 1 <= t + tiles * q <= bottom else None
-                for q in range(SLOTS)
-            ]
-            hh[s, :C, tile(t)] = halo_left(halo, owns)
-            hh[s, 2 * C :, tile(t)] = halo_right(halo, owns)
-
         pipeline(
             [
                 (0, top - 2, bottom + 2, stack_x),
@@ -398,54 +458,28 @@
                 (5, top, bottom, dot_second),
                 (6, top, bottom, dot_third),
                 (7, top, bottom, advance),
+                (top + 1, 0, len(beside), lambda i: beside[i]()),
             ],
             top - 2, bottom + 2,
         )
-        for t in range(tiles):
-            halo_h(t)
-        twist(hh, s)
-
-        def halo_second(i):
-            t, n = pieces[i]
-            second_u[i] = dot(w2, stack_halo(hh, s, t, n, ones[:, : n * TILE]))
-
-        def halo_third(i):
-            t, n = pieces[i]
-            hid, slope = activate(second_u.pop(i))
-            if s == 1:
-                p2h[:, t * TILE : (t + n) * TILE] = slope
-            third_u[i] = logits(hid.astype(BF16), n * TILE)
-
-        def halo_advance(i):
-            t, n = pieces[i]
-            t3 = jnp.tanh(third_u.pop(i))
-            if s == 1:
-                t3h[:, t * TILE : (t + n) * TILE] = t3
-            for i in range(n):
-                center = fh[s, :, tile(t + i)]
-                fh[s + 1, :, tile(t + i)] = center + 0.125 * wh[t + i] * change(
-                    t3[:, i * TILE : (i + 1) * TILE], center,
-                    [fh[s, :, tile(t + i + 1)], fh[s, :, tile(t + i - 1)], frh[s, t + i], flh[s, t + i]],
-                )
-
-        count = len(pieces)
-        pipeline(
-            [(0, 0, count, halo_second), (1, 0, count, halo_third), (2, 0, count, halo_advance)],
-            0, count,
-        )
-        twist(fh, s + 1)
-
-    forward(0, 4)
-    forward(1, 2)
-    for r in range(h):
-        final_ref[:, r, :] = fo[2, RIM + r]
-
+
+    arrive(slice(0, 1))
+    for t in range(tiles):
+        fh[0, :, tile(t)] = side_tile(t, right, left, lambda r: fo[0, r])
+    twist(fh, 0)
+    for stage in halo_input(0):
+        stage()
+    arrive(slice(1, None))
+    for t in range(tiles):
+        rest = side_tile(
+            t, right_rest, left_rest, lambda r: jnp.concatenate([widen(r), aim(r)], axis=0)
+        )
+        wh[t] = rest[:LEV]
+        th[t] = rest[LEV:]
+    for r in range(rows):
+        wo[r] = widen(r)
+    forward(0, 4, halo_step(0) + halo_input(1))
     fold = lambda v: sum(v[:, k * TILE : (k + 1) * TILE] for k in range(v.shape[1] // TILE))
-
-    for r in range(RIM - 2, RIM + h + 2):
-        ao[r] = wo[r] * (fo[2, r] - to[r])
-    for t in range(tiles):
-        ah[t] = wh[t] * (fh[2, :, tile(t)] - th[t])
 
     def errors(scaled, t3, center, others):
         e3 = jnp.concatenate([scaled * (other - center) for other in others], axis=0) * (1.0 - t3 * t3)
@@ -485,13 +519,30 @@
         if s == 0 or r in own_rows:
             sums[1] = sums[1] + fold(e1)
 
-    for t in range(tiles):
+    def halo_errors(t):
+        ah[t] = wh[t] * (fh[2, :, tile(t)] - th[t])
         lanes = slice(t * TILE, (t + 1) * TILE)
         _, e3b = errors(
             ah[t] * 0.0625, t3h[:, lanes], fh[1, :, tile(t)],
             [fh[1, :, tile(t + 1)], fh[1, :, tile(t - 1)], frh[1, t], flh[1, t]],
         )
-        eh[1, C : 2 * C, tile(t)] = (dot(w3t, e3b) * p2h[:, lanes]).astype(BF16)
+        e2b = (dot(w3t, e3b) * p2h[:, lanes]).astype(BF16)
+        eh[1, :, tile(t)] = jnp.concatenate(around(e2b), axis=0)
+
+    def halo_one(i):
+        t, n = pieces[i]
+        e1 = dot(w2t, stack_halo(eh, 1, t, n)) * p1h[1, :, t * TILE : (t + n) * TILE]
+        e1h[:, t * TILE : (t + n) * TILE] = e1.astype(BF16)
+
+    halo_back = [functools.partial(halo_errors, t) for t in range(tiles)]
+    halo_back += [lambda: twist(eh, 1)]
+    halo_back += [functools.partial(halo_one, i) for i in range(count)]
+    forward(1, 2, halo_step(1) + halo_back)
+    for r in range(h):
+        final_ref[:, r, :] = fo[2, RIM + r]
+
+    for r in range(RIM - 2, RIM + h + 2):
+        ao[r] = wo[r] * (fo[2, r] - to[r])
     top, bottom = RIM - 2, RIM + h + 2
     pipeline(
         [
@@ -502,19 +553,6 @@
         ],
         top, bottom,
     )
-    for t in range(tiles):
-        halo = eh[1, C : 2 * C, tile(t)]
-        owns = [
-            eo[1, C : 2 * C, at(t + tiles * q)] if top <= t + tiles * q < bottom else None
-            for q in range(SLOTS)
-        ]
-        eh[1, :C, tile(t)] = halo_left(halo, owns)
-        eh[1, 2 * C :, tile(t)] = halo_right(halo, owns)
-    twist(eh, 1)
-    for t, n in pieces:
-        e1 = dot(w2t, stack_halo(eh, 1, t, n)) * p1h[1, :, t * TILE : (t + n) * TILE]
-        e1h[:, t * TILE : (t + n) * TILE] = e1.astype(BF16)
-
     inner = slice(RIM * width, (RIM + h) * width)
 
     def shifted(ref, s):
@@ -579,43 +617,68 @@
 
     g2 = [acc2[a] + grad_two(0, a - 1) for a in range(3)]
     g3 = acc3[...] + dot_nt(e3o[0], h2o[0])
-    big = jnp.concatenate(g2 + [jnp.concatenate([g3, jnp.zeros((C - K, C), F32)], axis=0)], axis=1)
     chunk = grads_ref.shape[1]
-
-    def spread_rows(ref, v):
+    cuts = [(0, 4 * C), (4 * C, 4 * C), (8 * C, TILE), (10 * C, TILE)]
+
+    def spread_rows(i, v):
+        lo, n = cuts[i]
         for y in range(n_gy):
-            lo = y * chunk
-            ref[y] = v[lo : lo + chunk] if lo + chunk <= C else jnp.zeros((chunk, v.shape[1]), F32)
-
-    def to_peers(src, dst, send, recv, peers, key):
-        return [
+            at_row = y * chunk
+            inside_rows = at_row + chunk <= C
+            grads_ref[y, :, lo : lo + n] = (
+                v[at_row : at_row + chunk] if inside_rows else jnp.zeros((chunk, n), F32)
+            )
+
+    def to_peers(i, src, dst, send, recv, peers, key):
+        span = pl.ds(*cuts[i])
+        group = [
             pltpu.make_async_remote_copy(
-                src_ref=src(k, p), dst_ref=dst(k, p), send_sem=send.at[k], recv_sem=recv.at[k],
+                src_ref=src(k, p, span), dst_ref=dst(k, p, span),
+                send_sem=send.at[i * len(peers) + k], recv_sem=recv.at[i * len(peers) + k],
                 device_id=key(p), device_id_type=MESH,
             )
             for k, p in enumerate(peers)
         ]
-
-    def begin(group):
         for copy in group:
             copy.start()
         return group
 
-    along_y = lambda y: (gx, y)
-    along_x = lambda x: (x, gy)
-    spread_rows(grads_ref, big)
-    one = begin(to_peers(
-        lambda k, y: grads_ref.at[y], lambda k, y: got.at[k], send_one, recv_one, ys, along_y
-    ))
+    def scatter(i):
+        return to_peers(
+            i, lambda k, y, n: grads_ref.at[y, :, n], lambda k, y, n: got.at[k, :, n],
+            send_one, recv_one, ys, lambda y: (gx, y),
+        )
+
+    def cross(i):
+        return to_peers(
+            i, lambda k, x, n: part.at[:, n], lambda k, x, n: parts.at[gx, :, n],
+            send_two, recv_two, xs, lambda x: (x, gy),
+        )
+
+    def gather(i):
+        return to_peers(
+            i, lambda k, y, n: mine.at[:, n], lambda k, y, n: out_ref.at[gy, :, n],
+            send_three, recv_three, ys, lambda y: (gx, y),
+        )
+
+    spread_rows(0, jnp.concatenate([g2[0], g2[1][:, :C]], axis=1))
+    one = [scatter(0)]
+    spread_rows(1, jnp.concatenate([g2[1][:, C:], g2[2][:, : 2 * C]], axis=1))
+    one.append(scatter(1))
+    spread_rows(
+        2,
+        jnp.concatenate(
+            [g2[2][:, 2 * C :], jnp.concatenate([g3, jnp.zeros((C - K, C), F32)], axis=0)], axis=1
+        ),
+    )
+    one.append(scatter(2))
 
     for t in range(tiles):
         owns = [
             eo[0, C : 2 * C, at(t + tiles * q)] if RIM <= t + tiles * q < RIM + h else None
             for q in range(SLOTS)
         ]
-        eh[0, C : 2 * C, tile(t)] = nothing
-        eh[0, :C, tile(t)] = halo_left(nothing, owns)
-        eh[0, 2 * C :, tile(t)] = halo_right(nothing, owns)
+        eh[0, :, tile(t)] = jnp.concatenate([edge_left(owns), nothing, edge_right(owns)], axis=0)
     twist(eh, 0)
     for r in (RIM - 2, RIM - 1, RIM + h, RIM + h + 1):
         eo[0, :, at(r)] = jnp.zeros((3 * C, width), BF16)
@@ -643,62 +706,47 @@
     extra = pad16(
         jnp.concatenate([g1, total(sums[1]), total(sums[2]), tall(total(sums[3]))], axis=1), TILE
     )
-    spread_rows(extra_ref, extra)
-    four = begin(to_peers(
-        lambda k, y: extra_ref.at[y], lambda k, y: extra_got.at[k], send_four, recv_four, ys, along_y
-    ))
-
-    def gather_one(group, ref, arrived, here):
-        acc = ref[gy]
-        for k, copy in enumerate(group):
+    spread_rows(3, extra)
+    one.append(scatter(3))
+    two, three = [], []
+    for i, (lo, n) in enumerate(cuts):
+        span = slice(lo, lo + n)
+        acc = grads_ref[gy, :, span]
+        for k, copy in enumerate(one[i]):
             copy.wait_recv()
-            acc = acc + arrived[k]
-        here[...] = acc
-        return acc
-
-    def gather_two(group, ref, acc, to_send, out):
-        ref[gx] = acc
+            acc = acc + got[k, :, span]
+        part[:, span] = acc
+        two.append(cross(i))
+        parts[gx, :, span] = acc
+    for i, (lo, n) in enumerate(cuts):
+        span = slice(lo, lo + n)
+        for copy in two[i]:
+            copy.wait_recv()
+        acc = parts[0, :, span]
+        for x in range(1, n_gx):
+            acc = acc + parts[x, :, span]
+        acc = acc.astype(BF16)
+        mine[:, span] = acc
+        three.append(gather(i))
+        out_ref[gy, :, span] = acc
+    for group in three:
         for copy in group:
             copy.wait_recv()
-        acc = ref[0]
-        for x in range(1, n_gx):
-            acc = acc + ref[x]
-        acc = acc.astype(BF16)
-        to_send[...] = acc
-        out[gy] = acc
-
-    acc_big = gather_one(one, grads_ref, got, part)
-    two = begin(to_peers(
-        lambda k, x: part, lambda k, x: parts.at[gx], send_two, recv_two, xs, along_x
-    ))
-    acc_extra = gather_one(four, extra_ref, extra_got, extra_part)
-    five = begin(to_peers(
-        lambda k, x: extra_part, lambda k, x: extra_parts.at[gx], send_five, recv_five, xs, along_x
-    ))
-    gather_two(two, parts, acc_big, mine, out_ref)
-    three = begin(to_peers(
-        lambda k, y: mine, lambda k, y: out_ref.at[gy], send_three, recv_three, ys, along_y
-    ))
-    gather_two(five, extra_parts, acc_extra, extra_mine, rest_ref)
-    six = begin(to_peers(
-        lambda k, y: extra_mine, lambda k, y: rest_ref.at[gy], send_six, recv_six, ys, along_y
-    ))
-    for copy in three + six:
-        copy.wait_recv()
     for dx, dy, group in copies:
         @pl.when(exists(dx, dy))
         def _():
             for copy in group:
                 copy.wait_send()
-    for copy in one + two + three + four + five + six:
-        copy.wait_send()
-
-
-def finish_kernel(grads, rest, final, d1, d2, d3, ids, final_out, u1, u2, u3):
+    for group in one + two + three:
+        for copy in group:
+            copy.wait_send()
+
+
+def finish_kernel(grads, final, d1, d2, d3, ids, final_out, u1, u2, u3):
     final_out[...] = final[...]
     n_parts = C // grads.shape[1]
     big = jnp.concatenate([grads[y].astype(F32) for y in range(n_parts)], axis=0)
-    side = jnp.concatenate([rest[y].astype(F32) for y in range(n_parts)], axis=0)
+    side = big[:, 10 * C :]
     one = jnp.concatenate(
         [side[:, 4 * LEV * a : 4 * LEV * a + 3 * LEV] for a in range(3)]
         + [side[:, 12 * LEV : 12 * LEV + 1]],
@@ -744,11 +792,11 @@
     edge = (tiles + 2) * TILE
     shape = jax.ShapeDtypeStruct
     chunk = 8 * -(-C // (8 * n_gy))
-    wide = 10 * C
+    wide = 10 * C + TILE
     dma = pltpu.SemaphoreType.DMA
     vmem = pltpu.VMEM
-    over_y = [dma((n_gy - 1,)), dma((n_gy - 1,))]
-    over_x = [dma((n_gx - 1,)), dma((n_gx - 1,))]
+    over_y = [dma((4 * (n_gy - 1),))] * 2
+    over_x = [dma((4 * (n_gx - 1),))] * 2
 
     def sums(columns):
         return [
@@ -759,16 +807,15 @@
             vmem((chunk, columns), BF16),
         ]
 
-    final, summed, rest = pl.pallas_call(
+    final, summed = pl.pallas_call(
         functools.partial(fused_kernel, sizes),
         name="fused",
         out_shape=[
             shape(field.shape, F32),
             shape((n_gy, chunk, wide), BF16),
-            shape((n_gy, chunk, TILE), BF16),
         ],
         in_specs=[ANY] * 6,
-        out_specs=[VM] * 3,
+        out_specs=[VM] * 2,
         scratch_shapes=[
             vmem((3, rows, LEV, width), F32),
             vmem((3, LEV, edge), F32),
@@ -810,14 +857,15 @@
             vmem(conv_two.shape, F32),
             vmem(head.shape, F32),
             vmem((3, h, width), F32),
-            vmem((3, 3 * LEV, TILE), F32),
-            vmem((3, 3 * LEV, TILE), F32),
-            vmem((2, 3 * LEV, TILE), F32),
+            vmem((3, LEV, TILE), F32),
+            vmem((3, LEV, TILE), F32),
+            vmem((3, 2 * LEV, TILE), F32),
+            vmem((3, 2 * LEV, TILE), F32),
+            vmem((2, LEV, TILE), F32),
+            vmem((2, 2 * LEV, TILE), F32),
         ]
         + sums(wide)
-        + sums(TILE)
-        + [dma((6,)), dma((12,)), dma((12,))]
-        + over_y + over_x + over_y
+        + [dma((6,)), dma((18,)), dma((18,))]
         + over_y + over_x + over_y,
         compiler_params=pltpu.CompilerParams(
             collective_id=0, has_side_effects=True, vmem_limit_bytes=LIMIT
@@ -830,9 +878,9 @@
             shape(field.shape, F32),
             shape(conv_one.shape, F32), shape(conv_two.shape, F32), shape(head.shape, F32),
         ],
-        in_specs=[VM] * 7,
+        in_specs=[VM] * 6,
         out_specs=[VM] * 4,
-    )(summed, rest, final, d1, d2, d3, ids.reshape(1, -1))
+    )(summed, final, d1, d2, d3, ids.reshape(1, -1))
     return final, u1, u2, u3
 
 

time: 34.9 us -> 33.9 us (0.971)
  Pallas kernels: 34.1 us -> 33.1 us
    pallas_call x1, Pallas kernels: 31.9 us -> 31 us  [per_device(): pl.pallas_call(functools.partial(fused_kernel, sizes), name='fused', out_...]
where the time goes in v4:
time: 33.9 us; the launch traced here: 33.8 us
  Pallas kernels  33.1 us (98%)
  between operations  0.64 us (2%)
    pallas_call x1, Pallas kernels, per_device(): pl.pallas_call(functools.partial(fused_kernel, sizes), name='fused', out_...  31 us
    pallas_call x1, Pallas kernels, per_device(): pl.pallas_call(finish_kernel, name='update', out_shape=[shape(field.shape...  2.15 us

profile of v4, /device:TPU:0, one launch (start us, length us, event | category | flops | bytes accessed | tf_op | source)
XLA Modules:
  0.0 33.8 jit_solution(5574503842466201710)
XLA Ops:
  0.6 31.0 %fused.1 = (f32[8,8,256]{2,1,0:T(8,128)}, bf16[8,8,768]{2,1,0:T(8,128)(2,1)}) custom-call(f32[8,8,256]{2,1,0:T(8,128)} %field_in.1, f32[8,8,256]{2,1,0:T(8,128)} %target_in.1, s32[8,256]{1,0:T(8,128)} %mask_in.1, f32[64,73]{1,0:T(8,128)} %w1_in.1, f32[64,577]{1,0:T(8,128)} %w2_in.1, f32[32,65]{1,0:T(8,128)} %w3_in.1), custom_call_target="tpu_custom_call" | custom-call | tf_op jit(solution)/shard_map/fused/pallas_call | solution.py:810
  31.6 2.1 %update.1 = (f32[8,8,256]{2,1,0:T(8,128)}, f32[64,73]{1,0:T(8,128)}, f32[64,577]{1,0:T(8,128)}, f32[32,65]{1,0:T(8,128)}) custom-call(bf16[8,8,768]{2,1,0:T(8,128)(2,1)} %get-tuple-element.6.grads, f32[8,8,256]{2,1,0:T(8,128)} %get-tuple-element.7.final, f32[64,73]{1,0:T(8,128)} %d1.1, f32[64,577]{1,0:T(8,128)} %d2.1, f32[32,65]{1,0:T(8,128)} %d3.1, ...), custom_call_target="tpu_custom_call" | custom-call | tf_op jit(solution)/shard_map/update/pallas_call | solution.py:874

commit v5 on v4

--- a/solution.py
+++ b/solution.py
@@ -402,18 +402,18 @@
             ]
         return order + [lambda: twist(fh, s + 1)]
 
+    def own_input(s, r):
+        own = fo[s, r]
+        halo = fh[s, :, tile(r % tiles)]
+        before = own_left(own, halo, r // tiles)
+        after = own_right(own, halo, r // tiles)
+        fl[s, r] = before
+        fr[s, r] = after
+        xo[s, :, at(r)] = jnp.concatenate([before, own, after, unit], axis=0).astype(BF16)
+
     def forward(s, rad, beside):
         first_u, second_u, third_u = {}, {}, {}
         top, bottom = RIM - rad, RIM + h + rad
-
-        def stack_x(r):
-            own = fo[s, r]
-            halo = fh[s, :, tile(r % tiles)]
-            before = own_left(own, halo, r // tiles)
-            after = own_right(own, halo, r // tiles)
-            fl[s, r] = before
-            fr[s, r] = after
-            xo[s, :, at(r)] = jnp.concatenate([before, own, after, unit], axis=0).astype(BF16)
 
         def dot_first(r):
             first_u[r] = dot(w1, stack_own(xo, s, r))
@@ -452,7 +452,7 @@
 
         pipeline(
             [
-                (0, top - 2, bottom + 2, stack_x),
+                (0, top - 2, bottom + 2 if s else 0, lambda r: own_input(s, r)),
                 (2, top - 1, bottom + 1, dot_first),
                 (3, top - 1, bottom + 1, stack_h),
                 (5, top, bottom, dot_second),
@@ -467,8 +467,14 @@
     for t in range(tiles):
         fh[0, :, tile(t)] = side_tile(t, right, left, lambda r: fo[0, r])
     twist(fh, 0)
-    for stage in halo_input(0):
-        stage()
+    opening = halo_input(0)
+    pipeline(
+        [
+            (0, 0, len(opening), lambda i: opening[i]()),
+            (0, 0, rows, lambda r: own_input(0, r)),
+        ],
+        0, rows,
+    )
     arrive(slice(1, None))
     for t in range(tiles):
         rest = side_tile(
@@ -634,68 +640,77 @@
         group = [
             pltpu.make_async_remote_copy(
                 src_ref=src(k, p, span), dst_ref=dst(k, p, span),
-                send_sem=send.at[i * len(peers) + k], recv_sem=recv.at[i * len(peers) + k],
+                send_sem=send.at[i], recv_sem=recv.at[i],
                 device_id=key(p), device_id_type=MESH,
             )
             for k, p in enumerate(peers)
         ]
         for copy in group:
             copy.start()
-        return group
+
+    def settle(i, ref, sem):
+        span = pl.ds(*cuts[i])
+        pltpu.make_async_copy(ref.at[:, :, span], ref.at[:, :, span], sem.at[i]).wait()
 
     def scatter(i):
-        return to_peers(
+        to_peers(
             i, lambda k, y, n: grads_ref.at[y, :, n], lambda k, y, n: got.at[k, :, n],
             send_one, recv_one, ys, lambda y: (gx, y),
         )
 
     def cross(i):
-        return to_peers(
+        to_peers(
             i, lambda k, x, n: part.at[:, n], lambda k, x, n: parts.at[gx, :, n],
             send_two, recv_two, xs, lambda x: (x, gy),
         )
 
     def gather(i):
-        return to_peers(
+        to_peers(
             i, lambda k, y, n: mine.at[:, n], lambda k, y, n: out_ref.at[gy, :, n],
             send_three, recv_three, ys, lambda y: (gx, y),
         )
 
     spread_rows(0, jnp.concatenate([g2[0], g2[1][:, :C]], axis=1))
-    one = [scatter(0)]
+    scatter(0)
     spread_rows(1, jnp.concatenate([g2[1][:, C:], g2[2][:, : 2 * C]], axis=1))
-    one.append(scatter(1))
+    scatter(1)
     spread_rows(
         2,
         jnp.concatenate(
             [g2[2][:, 2 * C :], jnp.concatenate([g3, jnp.zeros((C - K, C), F32)], axis=0)], axis=1
         ),
     )
-    one.append(scatter(2))
-
-    for t in range(tiles):
+    scatter(2)
+
+    for r in (RIM - 2, RIM - 1, RIM + h, RIM + h + 1):
+        eo[0, :, at(r)] = jnp.zeros((3 * C, width), BF16)
+    g1 = {0: acc1[...]}
+
+    def edges(t):
         owns = [
             eo[0, C : 2 * C, at(t + tiles * q)] if RIM <= t + tiles * q < RIM + h else None
             for q in range(SLOTS)
         ]
         eh[0, :, tile(t)] = jnp.concatenate([edge_left(owns), nothing, edge_right(owns)], axis=0)
-    twist(eh, 0)
-    for r in (RIM - 2, RIM - 1, RIM + h, RIM + h + 1):
-        eo[0, :, at(r)] = jnp.zeros((3 * C, width), BF16)
-    g1 = acc1[...]
-    for t, n in pieces:
+
+    def edge_one(i):
+        t, n = pieces[i]
         e1 = dot(w2t, stack_halo(eh, 0, t, n)) * p1h[0, :, t * TILE : (t + n) * TILE]
         sums[1] = sums[1] + fold(e1)
-        g1 = g1 + dot_nt(e1.astype(BF16), stack_halo(xh, 0, t, n))
+        g1[0] = g1[0] + dot_nt(e1.astype(BF16), stack_halo(xh, 0, t, n))
+
+    closing = [functools.partial(edges, t) for t in range(tiles)]
+    closing += [lambda: twist(eh, 0)] + [functools.partial(edge_one, i) for i in range(count)]
     pipeline(
         [
             (0, low - 1, high + 1, lambda r: dot_back(0, r)),
             (1, low - 1, high + 1, lambda r: keep_one(0, r)),
+            (low - 1, 0, len(closing), lambda i: closing[i]()),
         ],
         low - 1, high + 1,
     )
     ring = h + 2
-    g1 = g1 + dot_nt(
+    g1 = g1[0] + dot_nt(
         e1o[0, :, (RIM - 1) * width : (RIM + h + 1) * width],
         jnp.concatenate(
             [xo[0, :, (RIM - 1 + a) * width : (RIM - 1 + a + ring) * width] for a in (-1, 0, 1)], axis=0
@@ -707,39 +722,41 @@
         jnp.concatenate([g1, total(sums[1]), total(sums[2]), tall(total(sums[3]))], axis=1), TILE
     )
     spread_rows(3, extra)
-    one.append(scatter(3))
-    two, three = [], []
+    scatter(3)
+    others_x = parts.at[pl.ds(0, n_gx - 1)]
+    others_y = out_ref.at[pl.ds(0, n_gy - 1)]
     for i, (lo, n) in enumerate(cuts):
         span = slice(lo, lo + n)
+        settle(i, got, recv_one)
         acc = grads_ref[gy, :, span]
-        for k, copy in enumerate(one[i]):
-            copy.wait_recv()
+        for k in range(n_gy - 1):
             acc = acc + got[k, :, span]
         part[:, span] = acc
-        two.append(cross(i))
+        cross(i)
         parts[gx, :, span] = acc
+    for dx, dy, group in copies:
+        @pl.when(exists(dx, dy))
+        def _():
+            for copy in group:
+                copy.wait_send()
+    for i in range(len(cuts)):
+        settle(i, got, send_one)
     for i, (lo, n) in enumerate(cuts):
         span = slice(lo, lo + n)
-        for copy in two[i]:
-            copy.wait_recv()
+        settle(i, others_x, recv_two)
         acc = parts[0, :, span]
         for x in range(1, n_gx):
             acc = acc + parts[x, :, span]
         acc = acc.astype(BF16)
         mine[:, span] = acc
-        three.append(gather(i))
+        gather(i)
         out_ref[gy, :, span] = acc
-    for group in three:
-        for copy in group:
-            copy.wait_recv()
-    for dx, dy, group in copies:
-        @pl.when(exists(dx, dy))
-        def _():
-            for copy in group:
-                copy.wait_send()
-    for group in one + two + three:
-        for copy in group:
-            copy.wait_send()
+    for i in range(len(cuts)):
+        settle(i, others_x, send_two)
+    for i in range(len(cuts)):
+        settle(i, others_y, recv_three)
+    for i in range(len(cuts)):
+        settle(i, others_y, send_three)
 
 
 def finish_kernel(grads, final, d1, d2, d3, ids, final_out, u1, u2, u3):
@@ -795,8 +812,8 @@
     wide = 10 * C + TILE
     dma = pltpu.SemaphoreType.DMA
     vmem = pltpu.VMEM
-    over_y = [dma((4 * (n_gy - 1),))] * 2
-    over_x = [dma((4 * (n_gx - 1),))] * 2
+    over_y = [dma((4,))] * 2
+    over_x = [dma((4,))] * 2
 
     def sums(columns):
         return [

time: 33.9 us -> 32.6 us (0.962)
  Pallas kernels: 33.1 us -> 31.8 us
    pallas_call x1, Pallas kernels: 31 us -> 29.7 us  [per_device(): pl.pallas_call(functools.partial(fused_kernel, sizes), name='fused', out_...]
where the time goes in v5:
time: 32.6 us; the launch traced here: 32.5 us
  Pallas kernels  31.8 us (98%)
  between operations  0.64 us (2%)
    pallas_call x1, Pallas kernels, per_device(): pl.pallas_call(functools.partial(fused_kernel, sizes), name='fused', out_...  29.7 us
    pallas_call x1, Pallas kernels, per_device(): pl.pallas_call(finish_kernel, name='update', out_shape=[shape(field.shape...  2.15 us

profile of v5, /device:TPU:0, one launch (start us, length us, event | category | flops | bytes accessed | tf_op | source)
XLA Modules:
  0.0 32.5 jit_solution(7208460349688296490)
XLA Ops:
  0.6 29.7 %fused.1 = (f32[8,8,256]{2,1,0:T(8,128)}, bf16[8,8,768]{2,1,0:T(8,128)(2,1)}) custom-call(f32[8,8,256]{2,1,0:T(8,128)} %field_in.1, f32[8,8,256]{2,1,0:T(8,128)} %target_in.1, s32[8,256]{1,0:T(8,128)} %mask_in.1, f32[64,73]{1,0:T(8,128)} %w1_in.1, f32[64,577]{1,0:T(8,128)} %w2_in.1, f32[32,65]{1,0:T(8,128)} %w3_in.1), custom_call_target="tpu_custom_call" | custom-call | tf_op jit(solution)/shard_map/fused/pallas_call | solution.py:827
  30.3 2.1 %update.1 = (f32[8,8,256]{2,1,0:T(8,128)}, f32[64,73]{1,0:T(8,128)}, f32[64,577]{1,0:T(8,128)}, f32[32,65]{1,0:T(8,128)}) custom-call(bf16[8,8,768]{2,1,0:T(8,128)(2,1)} %get-tuple-element.6.grads, f32[8,8,256]{2,1,0:T(8,128)} %get-tuple-element.7.final, f32[64,73]{1,0:T(8,128)} %d1.1, f32[64,577]{1,0:T(8,128)} %d2.1, f32[32,65]{1,0:T(8,128)} %d3.1, ...), custom_call_target="tpu_custom_call" | custom-call | tf_op jit(solution)/shard_map/update/pallas_call | solution.py:891

commit v6 on v5

--- a/solution.py
+++ b/solution.py
@@ -23,7 +23,8 @@
 BF16 = jnp.bfloat16
 VM = pl.BlockSpec(memory_space=pltpu.VMEM)
 ANY = pl.BlockSpec(memory_space=pl.ANY)
-LIMIT = 56 * 1024 * 1024
+LIMIT = 28 * 1024 * 1024
+SMALL = 8 * 1024 * 1024
 NT = (((1,), (1,)), ((), ()))
 
 
@@ -897,6 +898,7 @@
         ],
         in_specs=[VM] * 6,
         out_specs=[VM] * 4,
+        compiler_params=pltpu.CompilerParams(vmem_limit_bytes=SMALL),
     )(summed, final, d1, d2, d3, ids.reshape(1, -1))
     return final, u1, u2, u3
 

time: 32.6 us -> 36.6 us (1.12)
  local copies, waits for them, and re-layouts: 0 us -> 5.41 us
  Pallas kernels: 31.8 us -> 30.1 us
    unnamed x0 -> x20, local copies, waits for them, and re-layouts: none -> 5.41 us
    pallas_call x1, Pallas kernels: 2.15 us -> 1.13 us  [per_device(): pl.pallas_call(finish_kernel, name='update', out_shape=[shape(field.shape...]
    pallas_call x1, Pallas kernels: 29.7 us -> 28.9 us  [per_device(): pl.pallas_call(functools.partial(fused_kernel, sizes), name='fused', out_...]
where the time goes in v6:
time: 36.6 us; the launch traced here: 36.2 us
  Pallas kernels  30.1 us (82%)
  local copies, waits for them, and re-layouts  5.41 us (15%)
  between operations  0.69 us (2%)
    pallas_call x1, Pallas kernels, per_device(): pl.pallas_call(functools.partial(fused_kernel, sizes), name='fused', out_...  28.9 us
    unnamed x20, local copies, waits for them, and re-layouts  5.41 us
    pallas_call x1, Pallas kernels, per_device(): pl.pallas_call(finish_kernel, name='update', out_shape=[shape(field.shape...  1.13 us

profile of v6, /device:TPU:0, one launch (start us, length us, event | category | flops | bytes accessed | tf_op | source)
XLA Modules:
  0.0 36.2 jit_solution(14085193196642632025)
XLA Ops:
  0.6 0.0 copy-start
  0.6 0.9 %copy-done = f32[64,577]{1,0:T(8,128)S(1)} copy-done((f32[64,577]{1,0:T(8,128)S(1)}, f32[64,577]{1,0:T(8,128)}, u32[]{:S(2)}) %copy-start) | copy-done | bytes 147736
  1.6 0.0 copy-start.2
  1.6 0.8 %copy-done.2 = f32[8,8,256]{2,1,0:T(8,128)S(1)} copy-done((f32[8,8,256]{2,1,0:T(8,128)S(1)}, f32[8,8,256]{2,1,0:T(8,128)}, u32[]{:S(2)}) %copy-start.2) | copy-done | bytes 65560
  2.4 0.0 copy-start.3
  2.4 0.8 %copy-done.3 = f32[8,8,256]{2,1,0:T(8,128)S(1)} copy-done((f32[8,8,256]{2,1,0:T(8,128)S(1)}, f32[8,8,256]{2,1,0:T(8,128)}, u32[]{:S(2)}) %copy-start.3) | copy-done | bytes 65560
  3.2 0.0 copy-start.5
  3.2 0.8 %copy-done.5 = f32[64,73]{1,0:T(8,128)S(1)} copy-done((f32[64,73]{1,0:T(8,128)S(1)}, f32[64,73]{1,0:T(8,128)}, u32[]{:S(2)}) %copy-start.5) | copy-done | bytes 18712
  4.0 0.0 copy-start.6
  4.0 0.7 %copy-done.6 = f32[32,65]{1,0:T(8,128)S(1)} copy-done((f32[32,65]{1,0:T(8,128)S(1)}, f32[32,65]{1,0:T(8,128)}, u32[]{:S(2)}) %copy-start.6) | copy-done | bytes 8344
  4.7 0.0 copy-start.8
  4.7 0.7 %copy-done.8 = s32[8,256]{1,0:T(8,128)S(1)} copy-done((s32[8,256]{1,0:T(8,128)S(1)}, s32[8,256]{1,0:T(8,128)}, u32[]{:S(2)}) %copy-start.8) | copy-done | bytes 8216
  5.4 0.0 copy-start.1
  5.4 0.0 copy-start.4
  5.4 0.0 copy-start.7
  5.4 28.9 %fused.1 = (f32[8,8,256]{2,1,0:T(8,128)S(1)}, bf16[8,8,768]{2,1,0:T(8,128)(2,1)S(1)}) custom-call(f32[8,8,256]{2,1,0:T(8,128)S(1)} %copy-done.2, f32[8,8,256]{2,1,0:T(8,128)S(1)} %copy-done.3, s32[8,256]{1,0:T(8,128)S(1)} %copy-done.8, f32[64,73]{1,0:T(8,128)S(1)} %copy-done.5, f32[64,577]{1,0:T(8,128)S(1)} %copy-done, f32[32,65]{1,0:T(8,128)S(1)} %copy-done.6), custom_call_target="tpu_custom_call" | custom-call | tf_op jit(solution)/shard_map/fused/pallas_call | solution.py:828
  34.4 0.0 copy-start.9
  34.4 0.0 copy-done.1
  34.4 0.0 copy-done.4
  34.4 0.0 copy-done.7
  34.4 0.6 %copy-done.9 = s32[160]{0:T(256)S(1)} copy-done((s32[160]{0:T(256)S(1)}, s32[160]{0:T(256)}, u32[]{:S(2)}) %copy-start.9) | copy-done | bytes 664
  35.0 1.1 %update.1 = (f32[8,8,256]{2,1,0:T(8,128)}, f32[64,73]{1,0:T(8,128)}, f32[64,577]{1,0:T(8,128)}, f32[32,65]{1,0:T(8,128)}) custom-call(bf16[8,8,768]{2,1,0:T(8,128)(2,1)S(1)} %get-tuple-element.6.grads, f32[8,8,256]{2,1,0:T(8,128)S(1)} %get-tuple-element.7.final, f32[64,73]{1,0:T(8,128)S(1)} %copy-done.4, f32[64,577]{1,0:T(8,128)S(1)} %copy-done.1, ...), custom_call_target="tpu_custom_call" | custom-call | tf_op jit(solution)/shard_map/update/pallas_call | solution.py:892
Async XLA Ops:
  0.6 0.9 %copy-start = (f32[64,577]{1,0:T(8,128)S(1)}, f32[64,577]{1,0:T(8,128)}, u32[]{:S(2)}) copy-start(f32[64,577]{1,0:T(8,128)} %w2_in.1) | copy-start | bytes 443140
  1.6 0.8 %copy-start.2 = (f32[8,8,256]{2,1,0:T(8,128)S(1)}, f32[8,8,256]{2,1,0:T(8,128)}, u32[]{:S(2)}) copy-start(f32[8,8,256]{2,1,0:T(8,128)} %field_in.1) | copy-start | bytes 196612
  2.4 0.8 %copy-start.3 = (f32[8,8,256]{2,1,0:T(8,128)S(1)}, f32[8,8,256]{2,1,0:T(8,128)}, u32[]{:S(2)}) copy-start(f32[8,8,256]{2,1,0:T(8,128)} %target_in.1) | copy-start | bytes 196612
  3.2 0.8 %copy-start.5 = (f32[64,73]{1,0:T(8,128)S(1)}, f32[64,73]{1,0:T(8,128)}, u32[]{:S(2)}) copy-start(f32[64,73]{1,0:T(8,128)} %w1_in.1) | copy-start | bytes 56068
  4.0 0.7 %copy-start.6 = (f32[32,65]{1,0:T(8,128)S(1)}, f32[32,65]{1,0:T(8,128)}, u32[]{:S(2)}) copy-start(f32[32,65]{1,0:T(8,128)} %w3_in.1) | copy-start | bytes 24964
  4.7 0.7 %copy-start.8 = (s32[8,256]{1,0:T(8,128)S(1)}, s32[8,256]{1,0:T(8,128)}, u32[]{:S(2)}) copy-start(s32[8,256]{1,0:T(8,128)} %mask_in.1) | copy-start | bytes 24580
  5.4 29.0 %copy-start.1 = (f32[64,577]{1,0:T(8,128)S(1)}, f32[64,577]{1,0:T(8,128)}, u32[]{:S(2)}) copy-start(f32[64,577]{1,0:T(8,128)} %d2.1) | copy-start | bytes 443140
  5.4 29.0 %copy-start.4 = (f32[64,73]{1,0:T(8,128)S(1)}, f32[64,73]{1,0:T(8,128)}, u32[]{:S(2)}) copy-start(f32[64,73]{1,0:T(8,128)} %d1.1) | copy-start | bytes 56068
  5.4 29.0 %copy-start.7 = (f32[32,65]{1,0:T(8,128)S(1)}, f32[32,65]{1,0:T(8,128)}, u32[]{:S(2)}) copy-start(f32[32,65]{1,0:T(8,128)} %d3.1) | copy-start | bytes 24964
  34.4 0.7 %copy-start.9 = (s32[160]{0:T(256)S(1)}, s32[160]{0:T(256)}, u32[]{:S(2)}) copy-start(s32[160]{0:T(256)} %param.19) | copy-start | bytes 1924
